TPU v7x, 1024 devices: a whole 4x8x16 slice. The times are simulated.
1024 devices in a mesh: sub: 64 (over y, x, core), rep: 16 (over z).
Axes of the slice: x: 4, y: 8, z: 16, core: 2. Of those that a mesh axis runs over, the one named last changes fastest.
Arguments:
- dual_ops: bfloat16 [1024, 1024, 1024], P(('sub', 'rep'))
- mode_traces: float32 [1024, 6, 1024], P(('sub', 'rep')), may hold values from -0.046875 to 0.046875
- route: int32 [1024, 1024], P(('sub', 'rep')), may hold values from 0 to 1023, each once within a row
- mode_block: int32 [1024, 1], replicated, may hold values from 0 to 63
- local_gap: float32 [32, 1048576], P(None, ('sub', 'rep')), may hold values from -6 to 6
Outputs:
- multipliers: float32 [32, 1048576], P(None, ('sub', 'rep'))
- amplitudes: float32 [32, 384], replicated
Inputs may be any that keep to these rules, and one draw needn't show every extreme that they name: Each row of route lists every number below 1024 once. `mode_block`: every aggregate holds at least one subdomain.
All inputs are finite; a program needn't handle non-finite values.
Results may differ from a plain program's by a relative error of at most 0.003.
Values sent between devices are 32-bit elements; how exact they have to be, the bound alone decides.
A program may use at most 32 MiB of HBM per device.

v0:
```python
import jax
import jax.numpy as jnp
from jax import lax
from jax.sharding import PartitionSpec as P

MODES = 6
AGG_SUBS = 16
ITERS = 2


HIGHEST = lax.Precision.HIGHEST


def body(dual_ops, mode_traces, route, mode_block, local_gap):
    own_index = lax.axis_index("sub")
    plane_index = lax.axis_index("rep")
    peer_count = lax.axis_size("sub")
    plane_count = lax.axis_size("rep")
    operator = dual_ops[0]
    traces = mode_traces[0]
    slot_rows = route[0]
    rows_here = operator.shape[0]
    load_cases = local_gap.shape[0]
    per_peer = rows_here // peer_count
    blocks = mode_block[:, 0]
    block_count = blocks.shape[0] // AGG_SUBS
    coarse = block_count * MODES
    positions = jnp.arange(rows_here, dtype=jnp.int32)
    inverse = jnp.zeros((rows_here,), jnp.int32).at[slot_rows].set(positions)
    slot_peer = positions // per_peer
    within = positions % per_peer
    flip_index = jnp.where(
        slot_peer == own_index, slot_peer * per_peer + per_peer - 1 - within, positions
    )
    peer_ids = jnp.arange(peer_count, dtype=jnp.int32)
    peer_blocks = blocks[peer_ids * plane_count + plane_index]
    own_block = blocks[own_index * plane_count + plane_index]
    labels = jnp.arange(block_count, dtype=jnp.int32)
    peer_onehot = (peer_blocks[:, None] == labels[None, :]).astype(jnp.float32)
    own_onehot = (labels == own_block).astype(jnp.float32)
    trace_slots = traces[:, slot_rows]
    receive_index = flip_index[inverse]

    def to_peers(values):
        return values[:, slot_rows]

    def from_peers(values):
        return values[:, inverse]

    gap_peers = to_peers(local_gap)
    got_traces = lax.all_to_all(trace_slots, "sub", split_axis=1, concat_axis=1, tiled=True)
    got_gap = lax.all_to_all(gap_peers, "sub", split_axis=1, concat_axis=1, tiled=True)
    partner_traces = got_traces[:, flip_index]
    residual = local_gap - got_gap[:, receive_index]
    own_gram = jnp.dot(traces, traces.T, precision=HIGHEST)
    paired = (trace_slots[:, None, :] * partner_traces[None, :, :]).reshape(
        MODES, MODES, peer_count, per_peer
    )
    cross_terms = jnp.sum(paired, axis=3)
    cross_blocks = jnp.einsum("klq,qb->kbl", cross_terms, peer_onehot, precision=HIGHEST)
    own_blocks = own_gram[:, None, :] * own_onehot[None, :, None]
    row_term = 2.0 * (own_blocks - cross_blocks).reshape(MODES, coarse)
    gram_term = (own_onehot[:, None, None] * row_term[None]).reshape(coarse, coarse)

    def coarse_term(values):
        own_part = 2.0 * jnp.dot(values, traces.T, precision=HIGHEST)
        return (own_part[:, None, :] * own_onehot[None, :, None]).reshape(load_cases, coarse)

    def expand(amounts):
        grouped = amounts.reshape(load_cases, block_count, MODES)
        own_amounts = lax.dynamic_index_in_dim(grouped, own_block, 1, keepdims=False)
        own_part = jnp.dot(own_amounts, traces, precision=HIGHEST)
        peer_amounts = jnp.einsum("qb,rbk->rkq", peer_onehot, grouped, precision=HIGHEST)
        spread = jnp.repeat(peer_amounts, per_peer, axis=2)
        peer_part = jnp.sum(spread * partner_traces[None, :, :], axis=1)
        return own_part - from_peers(peer_part)

    squares = jnp.sum(residual * residual, axis=1)
    gram_matrix, coarse_res, norm_res = lax.psum(
        (gram_term, coarse_term(residual), squares), ("sub", "rep")
    )
    factor = jnp.linalg.cholesky(gram_matrix)

    def solve_coarse(right):
        return jax.scipy.linalg.cho_solve((factor, True), right.T).T

    amplitudes = solve_coarse(coarse_res)
    projected = residual - expand(amplitudes)
    inner_sum = norm_res - jnp.sum(amplitudes * coarse_res, axis=1)
    direction = projected
    multipliers = jnp.zeros_like(residual)
    for iteration in range(ITERS):
        product = lax.dot_general(
            direction.astype(jnp.bfloat16),
            operator,
            (((1,), (1,)), ((), ())),
            preferred_element_type=jnp.float32,
        )
        got_product = lax.all_to_all(
            to_peers(product), "sub", split_axis=1, concat_axis=1, tiled=True
        )
        image_jump = product - got_product[:, receive_index]
        coarse_jump, jump_squares, residual_cross, curvature = lax.psum(
            (
                coarse_term(image_jump),
                jnp.sum(image_jump * image_jump, axis=1),
                jnp.sum(residual * image_jump, axis=1),
                jnp.sum(direction * image_jump, axis=1),
            ),
            ("sub", "rep"),
        )
        step_size = inner_sum / curvature
        multipliers = multipliers + step_size[:, None] * direction
        residual = residual - step_size[:, None] * image_jump
        coarse_res = coarse_res - step_size[:, None] * coarse_jump
        norm_res = (
            norm_res - 2.0 * step_size * residual_cross + step_size * step_size * jump_squares
        )
        amplitudes = solve_coarse(coarse_res)
        if iteration + 1 < ITERS:
            projected = residual - expand(amplitudes)
            renewed = norm_res - jnp.sum(amplitudes * coarse_res, axis=1)
            direction = projected + (renewed / inner_sum)[:, None] * direction
            inner_sum = renewed
    return (multipliers, amplitudes)


def solution(mesh):
    placed = (
        P(("sub", "rep"), None, None),
        P(("sub", "rep"), None, None),
        P(("sub", "rep"), None),
        P(),
        P(None, ("sub", "rep")),
    )
    return jax.shard_map(
        body, mesh=mesh, in_specs=placed, out_specs=(P(None, ("sub", "rep")), P()), check_vma=False
    )
```

profile of v0, /device:TPU:1, one launch (start us, length us, event | category | flops | bytes accessed | tf_op | source)
XLA Modules:
  0.0 1061.6 jit_solution(10594613359692568682)
XLA Ops:
  9.0 2.8 gather_fusion.4
  13.0 18.2 %all-to-all-start.1 = ((f32[6,64,16]{2,0,1:T(8,128)}), f32[6,64,16]{2,0,1:T(8,128)S(1)}, u32[]{:S(2)}, u32[]{:S(2)}) async-start(f32[6,64,16]{2,0,1:T(8,128)} %copy.81), calls=%async_computation.1 | async-start | bytes 524288 | tf_op jit(solution)/shard_map/all_to_all | solution.py:51
  31.8 1.6 fusion.115
  34.6 4.3 scatter_custom_fusion
  39.0 8.8 gather_fusion.1
  54.1 4.0 gather_fusion
  58.1 1.9 reshape.376
  61.6 10.4 all-to-all-start
  72.5 4.0 gather_fusion.5
  85.6 1.8 reduce.20
  87.6 4.0 gather_fusion.2
  94.0 129.7 %psum.65 = f32[32,384]{1,0:T(8,128)} all-reduce(f32[32,384]{1,0:T(8,128)S(1)} %broadcast_multiply_fusion.3), channel_id=1, replica_groups=mesh['sub'=64,'rep'=16] {'sub','rep'}, use_global_device_ids=true, to_apply=%region_11.12 | all-reduce | flops 12288 | bytes 98304 | tf_op jit(solution)/shard_map/psum | solution.py:79
  223.6 340.2 %all-reduce.5.cloned.1.call-done = f32[384,384]{0,1:T(8,128)} async-done(((f32[384,384]{0,1:T(8,128)}), f32[384,384]{0,1:T(8,128)}) %all-reduce.5.cloned.1.call-update) | async-done | bytes 589840 | tf_op jit(solution)/shard_map/psum | solution.py:79
  567.1 11.7 %cholesky.77 = f32[128,128]{1,0:T(8,128)S(1)} custom-call(f32[128,128]{1,0:T(8,128)S(1)} %cholesky.192), custom_call_target="Cholesky" | custom-call | tf_op jit(solution)/shard_map/jit(cholesky)/cholesky | solution.py:82
  578.9 9.8 custom-call.24
  591.7 11.7 %cholesky.162 = f32[128,128]{1,0:T(8,128)S(1)} custom-call(f32[128,128]{1,0:T(8,128)S(1)} %cholesky.196), custom_call_target="Cholesky" | custom-call | tf_op jit(solution)/shard_map/jit(cholesky)/cholesky | solution.py:82
  603.5 10.0 custom-call.25
  615.7 11.7 %cholesky.181 = f32[128,128]{1,0:T(8,128)S(1)} custom-call(f32[128,128]{1,0:T(8,128)S(1)} %convolution_subtract_fusion.3), custom_call_target="Cholesky" | custom-call | tf_op jit(solution)/shard_map/jit(cholesky)/cholesky | solution.py:82
  631.9 8.2 while.6
  632.5 2.0 bitcast_dynamic-update-slice_fusion.2
  635.3 2.1 bitcast_dynamic-update-slice_fusion.2
  638.0 2.1 bitcast_dynamic-update-slice_fusion.2
  640.0 30.3 %custom-call.28 = f32[3,128,128]{1,2,0:T(8,128)S(1)} custom-call(f32[3,128,128]{2,1,0:T(8,128)} %get-tuple-element.23), custom_call_target="InvertDiagBlocksLowerTriangular" | custom-call | tf_op jit(solution)/shard_map/jit(_cho_solve)/triangular_solve | solution.py:85
  675.9 1.6 copy.88
  677.5 1.7 reshape.239
  679.2 1.3 fusion.12
  680.6 1.7 multiply_reduce_fusion.1
  682.3 2.0 copy.92
  684.3 5.4 gather_fusion.6
  689.7 1.9 copy.93
  691.5 1.5 fusion.6
  693.7 1.4 fusion.2
  695.1 1.9 copy.94
  697.0 5.4 gather_fusion.7
  702.4 1.9 reshape.378
  704.3 12.2 %all-to-all-start.2 = ((f32[64,1,512]{2,1,0:T(1,128)}), f32[64,1,512]{2,1,0:T(1,128)}, u32[]{:S(2)}, u32[]{:S(2)}) async-start(f32[64,1,512]{2,1,0:T(1,128)} %reshape.378), calls=%async_computation.2 | async-start | bytes 262144 | tf_op jit(solution)/shard_map/all_to_all | solution.py:99
  716.5 1.5 multiply_reduce_fusion.9
  718.0 9.3 all-to-all-done.2
  727.3 2.5 reduce.21
  729.8 1.9 reshape.379
  731.7 5.4 gather_fusion.8
  737.1 1.9 copy.95
  738.9 1.8 multiply_reduce_fusion.5
  743.0 1.7 mul.287
  744.7 1.7 copy.96
  746.3 1.4 broadcast_multiply_fusion.2
  747.8 117.1 %all-reduce.2 = (f32[32,384]{1,0:T(8,128)}, f32[32]{0:T(128)}, f32[32]{0:T(128)}, f32[32]{0:T(128)}, f32[32]{0:T(128)}) all-reduce(f32[32,384]{1,0:T(8,128)} %broadcast_multiply_fusion.2, f32[32]{0:T(128)} %get-tuple-element.29, f32[32]{0:T(128)} %get-tuple-element.28, ...), channel_id=1, replica_groups=mesh['sub'=64,'rep'=16] {'sub','rep'}, use_global_device_ids=true, to_apply=%region_20.22 | all-reduce | flops 12416 | bytes 99328 | tf_op jit(solution)/shard_map/psum | solution.py:103
  870.3 1.6 copy.97
  871.9 1.7 reshape.240
  874.9 1.7 multiply_reduce_fusion
  876.6 2.0 copy.100
  878.6 5.0 gather_fusion.9
  883.7 1.9 copy.101
  886.7 1.6 fusion.5
  890.7 5.0 gather_fusion.10
  895.8 1.9 reshape.380
  897.7 18.9 %all_to_all.45 = f32[64,1,512]{2,1,0:T(1,128)} all-to-all(f32[64,1,512]{2,1,0:T(1,128)} %reshape.380), channel_id=1, replica_groups=mesh['sub'=64,'rep'=16] {'sub'}, dimensions={0} | all-to-all | bytes 262144 | tf_op jit(solution)/shard_map/all_to_all | solution.py:99
  916.6 2.5 reduce.22
  919.1 1.9 reshape.381
  921.0 5.1 gather_fusion.11
  926.1 1.9 copy.103
  927.9 1.9 convolution_multiply_fusion
  931.2 117.3 %all-reduce.1 = (f32[32]{0:T(128)S(1)}, f32[32,384]{1,0:T(8,128)S(1)}) all-reduce(f32[32]{0:T(128)S(1)} %multiply_reduce_fusion.3, f32[32,384]{1,0:T(8,128)S(1)} %broadcast_multiply_fusion.1), channel_id=1, replica_groups=mesh['sub'=64,'rep'=16] {'sub','rep'}, use_global_device_ids=true, to_apply=%region_24.26 | all-reduce | flops 12320 | bytes 98560 | tf_op jit(solution)/shard_map/psum | solution.py:103
  1049.1 1.6 multiply_add_fusion
  (175 shorter events, 60.0 us)
Async XLA Ops:
  7.2 686.5 %copy-start = (bf16[1,1024,1024]{2,1,0:T(8,128)(2,1)S(1)}, bf16[1,1024,1024]{2,1,0:T(8,128)(2,1)}, u32[]{:S(2)}) copy-start(bf16[1,1024,1024]{2,1,0:T(8,128)(2,1)} %param.7) | copy-start | bytes 6291460
  8.0 46.1 %copy-start.17 = (s32[1024]{0:T(1024)}, s32[1024]{0:T(1024)S(1)}, u32[]{:S(2)}) copy-start(s32[1024]{0:T(1024)S(1)} %broadcast_clamp_fusion.2) | copy-start | bytes 12292
  13.0 48.6 %all-to-all-start.1 = ((f32[6,64,16]{2,0,1:T(8,128)}), f32[6,64,16]{2,0,1:T(8,128)S(1)}, u32[]{:S(2)}, u32[]{:S(2)}) async-start(f32[6,64,16]{2,0,1:T(8,128)} %copy.81), calls=%async_computation.1 | async-start | bytes 524288 | tf_op jit(solution)/shard_map/all_to_all | solution.py:51
  38.9 8.9 copy-start.21
  38.9 9.6 copy-start.1
  39.0 15.0 %copy-start.11 = (f32[32,1024]{1,0:T(8,128)S(1)}, f32[32,1024]{1,0:T(8,128)}, u32[]{:S(2)}) copy-start(f32[32,1024]{1,0:T(8,128)} %param.11) | copy-start | bytes 393220
  48.5 39.1 %copy-start.19 = (s32[1024]{0:T(1024)}, s32[1024]{0:T(1024)S(1)}, u32[]{:S(2)}) copy-start(s32[1024]{0:T(1024)S(1)} %broadcast_clamp_fusion.1) | copy-start | bytes 12292
  51.8 20.7 %copy-start.25 = (s32[1024]{0:T(1024)S(1)}, s32[1024]{0:T(1024)}, u32[]{:S(2)}) copy-start(s32[1024]{0:T(1024)} %broadcast_clamp_fusion) | copy-start | bytes 12292
  61.6 18.2 %copy-start.26 = (s32[64]{0:T(128)}, s32[64]{0:T(128)S(1)}, u32[]{:S(2)}) copy-start(s32[64]{0:T(128)S(1)} %gather_fusion.3) | copy-start | bytes 772
  61.6 22.8 %all-to-all-start = ((f32[64,1,512]{2,1,0:T(1,128)}), f32[64,1,512]{2,1,0:T(1,128)S(1)}, u32[]{:S(2)}, u32[]{:S(2)}) async-start(f32[64,1,512]{2,1,0:T(1,128)} %reshape.376), calls=%async_computation | async-start | bytes 262144 | tf_op jit(solution)/shard_map/all_to_all | solution.py:52
  72.0 491.9 %all-reduce.5.cloned.1.call-start = ((), (), s32[]{:S(2)}) async-start(), calls=%async_computation.4 | async-start | bytes 1179648 | tf_op jit(solution)/shard_map/psum | solution.py:79
  77.8 1.9 copy-start.9
  77.8 5.6 copy-start.23
  83.4 9.4 copy-start.12
  84.3 0.7 copy-start.14
  566.3 0.8 copy-start.7
  567.1 64.7 %copy-start.28 = (s32[3]{0:T(128)S(1)}, s32[3]{0:T(128)}, u32[]{:S(2)}) copy-start(s32[3]{0:T(128)} %iota_multiply_fusion) | copy-start | bytes 40
  591.1 0.7 copy-start.13
  627.4 3.3 copy-start.4
  674.1 0.6 copy-start.15
  674.7 0.6 copy-start.16
  693.0 0.7 copy-start.2
  704.3 23.0 %all-to-all-start.2 = ((f32[64,1,512]{2,1,0:T(1,128)}), f32[64,1,512]{2,1,0:T(1,128)}, u32[]{:S(2)}, u32[]{:S(2)}) async-start(f32[64,1,512]{2,1,0:T(1,128)} %reshape.378), calls=%async_computation.2 | async-start | bytes 262144 | tf_op jit(solution)/shard_map/all_to_all | solution.py:99
  731.7 14.6 %copy-start.24 = (f32[384]{0:T(512)S(1)}, f32[384]{0:T(512)}, u32[]{:S(2)}) copy-start(f32[384]{0:T(512)} %mul.247) | copy-start | bytes 4612
  740.7 0.6 copy-start.8
  740.7 132.9 %copy-start.27 = (s32[64]{0:T(128)S(1)}, s32[64]{0:T(128)}, u32[]{:S(2)}) copy-start(s32[64]{0:T(128)} %copy-done.26) | copy-start | bytes 772
  746.3 132.3 %copy-start.22 = (s32[1024]{0:T(1024)S(1)}, s32[1024]{0:T(1024)}, u32[]{:S(2)}) copy-start(s32[1024]{0:T(1024)} %copy-done.21) | copy-start | bytes 12292
  867.0 2.0 copy-start.10
  886.7 4.0 copy-start.18
  888.4 0.6 copy-start.5
  889.7 29.4 %copy-start.6 = (f32[32,1024]{1,0:T(8,128)}, f32[32,1024]{1,0:T(8,128)S(1)}, u32[]{:S(2)}) copy-start(f32[32,1024]{1,0:T(8,128)S(1)} %fusion) | copy-start | bytes 393220
  889.7 31.3 %copy-start.20 = (s32[1024]{0:T(1024)S(1)}, s32[1024]{0:T(1024)}, u32[]{:S(2)}) copy-start(s32[1024]{0:T(1024)} %copy-done.19) | copy-start | bytes 12292
  921.0 128.1 %copy-start.3 = (f32[32,1024]{1,0:T(8,128)S(1)}, f32[32,1024]{1,0:T(8,128)}, u32[]{:S(2)}) copy-start(f32[32,1024]{1,0:T(8,128)} %copy-done.2) | copy-start | bytes 393220
Sparse Core Ops, SparseCore 0:
  84.4 479.3 all-reduce.4
where the time goes:
time: 1070 us; the launch traced here: 1060 us
  blocking collectives  383 us (36%)
  waiting for transfers between devices  350 us (33%)
  local copies, waits for them, and re-layouts  122 us (11%)
  other arithmetic  120 us (11%)
  starting transfers between devices  40.8 us (4%)
  matrix products  26.6 us (2%)
  between operations  19.1 us (2%)
    psum x1, waiting for transfers between devices, body(): lax.psum((gram_term, coarse_term(residual), squares), ('sub', 'rep'))  340 us
    psum x2, blocking collectives, body(): lax.psum((coarse_term(image_jump), jnp.sum(image_jump * image_jump, axis=...  234 us
    psum x1, blocking collectives, body(): lax.psum((gram_term, coarse_term(residual), squares), ('sub', 'rep'))  130 us
    another operation x10, other arithmetic, body(): factor = jnp.linalg.cholesky(gram_matrix)  56.4 us
    another operation x4, other arithmetic, solve_coarse(): return jax.scipy.linalg.cho_solve((factor, True), right.T).T  32 us
  transfers between devices with their start and end apart: 4, of which 2 were waited for; matrix products, arithmetic and copies ran while one was open for 5% of the time, Pallas kernels for 0%

commit v1 on v0

v1 whole, which is shorter than its diff:
```python
import jax
import jax.numpy as jnp
from jax import lax
from jax.experimental import pallas as pl
from jax.experimental.pallas import tpu as pltpu
from jax.sharding import PartitionSpec as P

SUB = 64
REP = 16
PER = 16
ROWS = 1024
CASES = 32
MODES = 6
AGGS = 64
NC = 384
TILES = 16
SLICE = 24
HALF = 24
F32 = jnp.float32
BF16 = jnp.bfloat16
HIGHEST = lax.Precision.HIGHEST
MESH = pl.DeviceIdType.MESH


def nt(left, right, precision=None):
    return lax.dot_general(
        left, right, (((1,), (1,)), ((), ())), precision=precision, preferred_element_type=F32
    )


def nn(left, right, precision=None):
    return lax.dot_general(
        left, right, (((1,), (0,)), ((), ())), precision=precision, preferred_element_type=F32
    )


def split(values):
    high = values.astype(BF16)
    rest = values - high.astype(F32)
    middle = rest.astype(BF16)
    low = (rest - middle.astype(F32)).astype(BF16)
    return high, middle, low


def permuted(values, onehot, product):
    high, middle, low = split(values)
    return (product(high, onehot) + product(middle, onehot)) + product(low, onehot)


def iota(shape, dim):
    return lax.broadcasted_iota(jnp.int32, shape, dim)


def greet(own, plane):
    barrier = pltpu.get_barrier_semaphore()

    def over_sub(i, _):
        pl.semaphore_signal(
            barrier, inc=1, device_id=(lax.rem(own + i, SUB), plane), device_id_type=MESH
        )
        return 0

    def over_rep(i, _):
        pl.semaphore_signal(
            barrier, inc=1, device_id=(own, lax.rem(plane + i, REP)), device_id_type=MESH
        )
        return 0

    lax.fori_loop(1, SUB, over_sub, 0)
    lax.fori_loop(1, REP, over_rep, 0)
    return barrier


def to_peer(source, target, send, receive, peer, plane):
    return pltpu.make_async_remote_copy(
        src_ref=source,
        dst_ref=target,
        send_sem=send,
        recv_sem=receive,
        device_id=(peer, plane),
        device_id_type=MESH,
    )


def pack(values, message_ref):
    wide = jnp.concatenate([values, jnp.zeros((64, ROWS), F32)], axis=0)
    tall = jnp.transpose(wide).reshape(SUB, 2, 8, 128)
    message_ref[...] = tall[:, 0] + pltpu.roll(tall[:, 1], 64, 2)


def unpack(landed_ref):
    tiles = landed_ref[...]
    low = iota((SUB, 8, 128), 2) < 64
    first = jnp.where(low, tiles, 0.0)
    second = jnp.where(low, pltpu.roll(tiles, 64, 2), 0.0)
    tall = jnp.stack([first, second], axis=1).reshape(ROWS, 128)
    return jnp.transpose(tall)[:64]


def flip_own(message_ref, landed_ref, own):
    tile = pltpu.roll(message_ref[own], 64, 1)
    for a in range(8):
        landed_ref[own, pl.ds(7 - a, 1), :] = tile[a : a + 1, :]


def exchange_start(message_ref, landed_ref, send, receive, own, plane):
    def one(i, _):
        peer = lax.rem(own + i, SUB)
        to_peer(
            message_ref.at[peer], landed_ref.at[own], send.at[peer], receive.at[own], peer, plane
        ).start()
        return 0

    lax.fori_loop(1, SUB, one, 0)


def exchange_wait(message_ref, landed_ref, send, receive, own, plane):
    def one(i, _):
        peer = lax.rem(own + i, SUB)
        to_peer(
            message_ref.at[peer], landed_ref.at[peer], send.at[peer], receive.at[peer], peer, plane
        ).wait_recv()
        return 0

    lax.fori_loop(1, SUB, one, 0)


def exchange_sent(message_ref, landed_ref, send, receive, own, plane):
    def one(i, _):
        peer = lax.rem(own + i, SUB)
        to_peer(
            message_ref.at[peer], landed_ref.at[peer], send.at[peer], receive.at[peer], peer, plane
        ).wait_send()
        return 0

    lax.fori_loop(1, SUB, one, 0)


def spread_start(piece_ref, landed_ref, index, send, receive, own, plane):
    def one(i, _):
        peer = lax.rem(own + i, SUB)
        to_peer(
            piece_ref, landed_ref.at[index], send.at[peer], receive.at[index], peer, plane
        ).start()
        return 0

    lax.fori_loop(1, SUB, one, 0)


def spread_sent(piece_ref, landed_ref, index, send, receive, own, plane):
    def one(i, _):
        peer = lax.rem(own + i, SUB)
        to_peer(
            piece_ref, landed_ref.at[index], send.at[peer], receive.at[index], peer, plane
        ).wait_send()
        return 0

    lax.fori_loop(1, SUB, one, 0)


def column(piece_ref, landed_ref, send, receive, own, plane, act):
    def one(i, _):
        other = lax.rem(plane + i, REP)
        if act == "start":
            to_peer(
                piece_ref, landed_ref.at[plane], send.at[other], receive.at[plane], own, other
            ).start()
        elif act == "recv":
            to_peer(
                piece_ref, landed_ref.at[other], send.at[other], receive.at[other], own, other
            ).wait_recv()
        else:
            to_peer(
                piece_ref, landed_ref.at[other], send.at[other], receive.at[other], own, other
            ).wait_send()
        return 0

    lax.fori_loop(1, REP, one, 0)


def setup_kernel(
    operator_ref, traces_ref, route_ref, blocks_ref, gap_ref,
    residual_ref, basis_ref, glued_ref, onehot_ref, gram_ref, coarse_ref, norm_ref,
    message, landed, rows_ref, half_ref, pair_ref, even_ref,
    gram_out, gram_in, part_ref, column_in, total_ref, gathered,
    send_a, receive_a, send_b, receive_b, send_c, receive_c, send_d, receive_d,
):
    own = lax.axis_index("sub")
    plane = lax.axis_index("rep")
    barrier = greet(own, plane)

    route_row = route_ref[...]
    wide_route = jnp.broadcast_to(route_row, (128, ROWS)).astype(F32)

    @pl.loop(0, 4)
    def _(step):
        rows = pl.ds(pl.multiple_of(step * 256, 256), 256)
        hit = iota((256, ROWS), 0) + step * 256 == route_row
        onehot_ref[rows, :] = hit.astype(F32).astype(BF16)

    stacked = jnp.concatenate(
        [gap_ref[...], traces_ref[0], jnp.zeros((2, ROWS), F32)], axis=0
    )
    ordered = permuted(stacked, onehot_ref[...], nn)
    pack(jnp.concatenate([ordered, jnp.zeros((24, ROWS), F32)], axis=0), message)

    pl.semaphore_wait(barrier, SUB - 1 + REP - 1)
    exchange_start(message, landed, send_a, receive_a, own, plane)
    flip_own(message, landed, own)

    tall_route = jnp.transpose(wide_route)
    for tile in range(8):
        hit = tall_route == (iota((ROWS, 128), 1) + tile * 128).astype(F32)
        rows_ref[:, tile * 128 : tile * 128 + 128] = hit.astype(F32).astype(BF16)

    @pl.loop(0, 4)
    def _(step):
        rows = pl.ds(pl.multiple_of(step * 256, 256), 256)
        half_ref[rows, :] = nn(operator_ref[0, rows, :], onehot_ref[...]).astype(BF16)

    @pl.loop(0, 4)
    def _(step):
        rows = pl.ds(pl.multiple_of(step * 256, 256), 256)
        glued_ref[rows, :] = nn(rows_ref[rows, :], half_ref[...]).astype(BF16)

    blocks = blocks_ref[...].astype(F32)
    picked = jnp.where(iota((SUB, REP), 1) == plane, blocks, 0.0)
    peer_block = jnp.sum(picked, axis=1, keepdims=True)
    hit = peer_block == iota((SUB, 128), 1).astype(F32)
    by_peer = jnp.concatenate([hit.astype(F32), jnp.zeros((64, 128), F32)], axis=0)
    by_block = jnp.transpose(by_peer)
    repeat = (iota((128, ROWS), 1) // PER == iota((128, ROWS), 0)).astype(F32).astype(BF16)
    peer_mask = nn(by_block[:AGGS].astype(BF16), repeat)
    own_mask = jnp.sum(
        jnp.where(iota((AGGS, 128), 1) == own, by_block[:AGGS], 0.0), axis=1, keepdims=True
    )
    traces = ordered[CASES : CASES + 8]
    pair_ref[...] = jnp.zeros_like(pair_ref)
    even_ref[...] = jnp.zeros_like(even_ref)
    for k in range(MODES):
        row = traces[k : k + 1]
        at = k // 2 + HALF * (k % 2)
        even_ref[at : at + 1, :] = row
        lane = (18, 42, 19)[k // 2]
        pair_ref[k % 2, lane : lane + 1, :] = row

    exchange_wait(message, landed, send_a, receive_a, own, plane)
    partner = unpack(landed)
    residual = ordered[:CASES] - partner[:CASES]
    residual_ref[...] = residual
    for k in range(MODES):
        basis_ref[64 * k : 64 * k + 64, :] = (
            own_mask * traces[k : k + 1] - peer_mask * partner[CASES + k : CASES + k + 1]
        )
    crossed = 2.0 * nt(basis_ref[...], even_ref[...], HIGHEST)
    outgoing = crossed[:64]
    for k in range(1, MODES):
        outgoing = outgoing + pltpu.roll(crossed[64 * k : 64 * k + 64], 3 * k, 1)
    first = 2.0 * nt(residual, pair_ref[0], HIGHEST)
    second = 2.0 * nt(residual, pair_ref[1], HIGHEST)
    squares = jnp.sum(residual * residual, axis=1, keepdims=True)
    first = jnp.where(iota((CASES, 128), 1) == 43, squares, first)
    gram_out[...] = (outgoing + jnp.concatenate([first, second], axis=0)).reshape(SUB, 1, 128)

    exchange_start(gram_out, gram_in, send_b, receive_b, own, plane)
    gram_in[own] = gram_out[own]
    exchange_sent(message, landed, send_a, receive_a, own, plane)
    exchange_wait(gram_out, gram_in, send_b, receive_b, own, plane)
    arrived = gram_in[...].reshape(SUB, 128)
    turned = jnp.transpose(jnp.concatenate([arrived, jnp.zeros((64, 128), F32)], axis=0))
    grouped = nn(turned[: 2 * HALF], by_peer, HIGHEST)
    part_ref[...] = grouped[:HALF] + pltpu.roll(grouped[HALF:], 64, 1)

    column(part_ref, column_in, send_c, receive_c, own, plane, "start")
    column_in[plane] = part_ref[...]
    exchange_sent(gram_out, gram_in, send_b, receive_b, own, plane)
    column(part_ref, column_in, send_c, receive_c, own, plane, "recv")
    total_ref[...] = jnp.sum(column_in[...], axis=0)

    spread_start(total_ref, gathered, own, send_d, receive_d, own, plane)
    gathered[own] = total_ref[...]
    column(part_ref, column_in, send_c, receive_c, own, plane, "sent")
    exchange_wait(gathered, gathered, send_d, receive_d, own, plane)
    for k in range(MODES):
        for j in range(3):
            gram_ref[64 * k : 64 * k + 64, 128 * j : 128 * j + 128] = gathered[:, 3 * k + j, :]
    near = gathered[:, 18, :]
    far = gathered[:, 19, :]
    even_odd = (near, pltpu.roll(near, 64, 1), far)
    lower = iota((CASES, 128), 1) < 64
    for i in range(3):
        coarse_ref[:, 128 * i : 128 * i + 128] = jnp.where(
            lower, even_odd[i][:CASES], pltpu.roll(even_odd[i][CASES:], 64, 1)
        )
    totals = jnp.sum(jnp.where(iota((CASES, 128), 1) >= 64, far[:CASES], 0.0), axis=1, keepdims=True)
    norm_ref[...] = jnp.broadcast_to(totals, (CASES, 128))
    spread_sent(total_ref, gathered, own, send_d, receive_d, own, plane)


def invert_kernel(gram_ref, inverse_ref):
    inverse_ref[...] = gram_ref[...]
    lane = iota((128, 128), 1)
    line = iota((128, 128), 0)

    @pl.loop(0, 3)
    def _(block):
        at = pl.ds(pl.multiple_of(block * 128, 128), 128)
        pivot = inverse_ref[at, at]
        for k in range(128):
            scale = 1.0 / pivot[k : k + 1, k : k + 1]
            row = jnp.where(lane[:1] == k, scale, pivot[k : k + 1, :] * scale)
            left = pivot[:, k : k + 1]
            kept = jnp.where(lane == k, 0.0, pivot)
            pivot = jnp.where(line == k, row, kept - left * row)
        rows = nn(pivot, inverse_ref[at, :], HIGHEST)
        lefts = inverse_ref[:, at]
        mine = iota((NC, 128), 0) // 128 == block
        lefts = jnp.where(mine, 0.0, lefts)
        inverse_ref[...] = inverse_ref[...] - nn(lefts, rows, HIGHEST)
        inverse_ref[:, at] = -nn(lefts, pivot, HIGHEST)
        inverse_ref[at, :] = rows
        inverse_ref[at, at] = pivot


def owner_of(tile):
    return 4 * tile + lax.rem(tile, 4)


def reduce_start(pay, first_in, send, receive, own, plane):
    def one(tile, _):
        peer = owner_of(tile)

        @pl.when(peer != own)
        def _():
            to_peer(
                pay.at[tile], first_in.at[own], send.at[tile], receive.at[own], peer, plane
            ).start()

        return 0

    lax.fori_loop(0, TILES, one, 0)


def reduce_middle(pay, first_in, mid, second_in, last, result, sems, own, plane):
    send_1, receive_1, send_2, receive_2, send_3, receive_3 = sems
    tile = own // 4

    @pl.when(lax.rem(own, 4) == lax.rem(tile, 4))
    def _():
        first_in[own] = pay[tile]

        def one(i, _):
            peer = lax.rem(own + i, SUB)
            to_peer(
                pay.at[tile], first_in.at[peer], send_1.at[tile], receive_1.at[peer], peer, plane
            ).wait_recv()
            return 0

        lax.fori_loop(1, SUB, one, 0)
        mid[...] = jnp.sum(first_in[...], axis=0)
        column(mid, second_in, send_2, receive_2, own, plane, "start")
        second_in[plane] = mid[...]
        column(mid, second_in, send_2, receive_2, own, plane, "recv")
        last[...] = jnp.sum(second_in[...], axis=0)
        spread_start(last, result, tile, send_3, receive_3, own, plane)
        result[tile] = last[...]


def reduce_finish(pay, first_in, mid, second_in, last, result, sems, own, plane):
    send_1, receive_1, send_2, receive_2, send_3, receive_3 = sems

    def one(tile, _):
        peer = owner_of(tile)

        @pl.when(peer != own)
        def _():
            to_peer(
                last, result.at[tile], send_3.at[peer], receive_3.at[tile], peer, plane
            ).wait_recv()

        return 0

    lax.fori_loop(0, TILES, one, 0)


def reduce_sent(pay, first_in, mid, second_in, last, result, sems, own, plane):
    send_1, receive_1, send_2, receive_2, send_3, receive_3 = sems

    def one(tile, _):
        peer = owner_of(tile)

        @pl.when(peer != own)
        def _():
            to_peer(
                pay.at[tile], first_in.at[own], send_1.at[tile], receive_1.at[own], peer, plane
            ).wait_send()

        return 0

    lax.fori_loop(0, TILES, one, 0)
    tile = own // 4

    @pl.when(lax.rem(own, 4) == lax.rem(tile, 4))
    def _():
        column(mid, second_in, send_2, receive_2, own, plane, "sent")
        spread_sent(last, result, tile, send_3, receive_3, own, plane)


def load_pay(pay, sums, scalars):
    extra = jnp.zeros((CASES, 128), F32)
    for at, value in enumerate(scalars):
        extra = jnp.where(iota((CASES, 128), 1) == at, value, extra)
    for i in range(4):
        for j in range(3):
            pay[4 * i + j] = sums[8 * i : 8 * i + 8, 128 * j : 128 * j + 128]
        pay[4 * i + 3] = extra[8 * i : 8 * i + 8]


def read_result(result):
    columns = []
    for j in range(4):
        columns.append(jnp.concatenate([result[4 * i + j] for i in range(4)], axis=0))
    return jnp.concatenate(columns[:3], axis=1), columns[3]


def row_sum(values):
    return jnp.sum(values, axis=1, keepdims=True)


def solve_kernel(
    residual_ref, basis_ref, glued_ref, onehot_ref, inverse_ref, coarse_ref, norm_ref,
    multipliers_ref, amplitudes_ref,
    message, landed, pay_a, first_a, mid_a, second_a, last_a, result_a,
    pay_b, first_b, mid_b, second_b, last_b, result_b,
    send_x, receive_x,
    send_a1, receive_a1, send_a2, receive_a2, send_a3, receive_a3,
    send_b1, receive_b1, send_b2, receive_b2, send_b3, receive_b3,
):
    own = lax.axis_index("sub")
    plane = lax.axis_index("rep")
    barrier = greet(own, plane)
    round_a = (pay_a, first_a, mid_a, second_a, last_a, result_a,
               (send_a1, receive_a1, send_a2, receive_a2, send_a3, receive_a3), own, plane)
    round_b = (pay_b, first_b, mid_b, second_b, last_b, result_b,
               (send_b1, receive_b1, send_b2, receive_b2, send_b3, receive_b3), own, plane)

    residual = residual_ref[...]
    coarse = coarse_ref[...]
    start = nn(coarse, inverse_ref[...], HIGHEST)
    direction = residual - nn(start, basis_ref[...], HIGHEST)
    inner = norm_ref[:, :1] - row_sum(start * coarse)
    product = nt(direction.astype(BF16), glued_ref[...])
    pack(jnp.concatenate([product, jnp.zeros((32, ROWS), F32)], axis=0), message)
    load_pay(pay_a, 2.0 * nt(product, basis_ref[...], HIGHEST), (2.0 * row_sum(direction * product),))

    pl.semaphore_wait(barrier, SUB - 1 + REP - 1)
    reduce_start(pay_a, first_a, send_a1, receive_a1, own, plane)
    exchange_start(message, landed, send_x, receive_x, own, plane)
    flip_own(message, landed, own)
    reduce_middle(*round_a)
    exchange_wait(message, landed, send_x, receive_x, own, plane)
    jumped = product - unpack(landed)[:CASES]
    reduce_finish(*round_a)

    coarse_jump, sums = read_result(result_a)
    curvature = sums[:, 0:1]
    step = inner / curvature
    coarse_next = coarse - step * coarse_jump
    amplitudes = nn(coarse_next, inverse_ref[...], HIGHEST)
    projected = (residual - step * jumped) - nn(amplitudes, basis_ref[...], HIGHEST)
    high, low, _ = split(projected)
    both = nt(jnp.concatenate([high, low], axis=0), glued_ref[...])
    image = both[:CASES] + both[CASES:]
    load_pay(
        pay_b,
        2.0 * nt(image, basis_ref[...], HIGHEST),
        (
            2.0 * row_sum(projected * image),
            2.0 * row_sum(projected * product) + 2.0 * row_sum(direction * image),
            row_sum(projected * projected),
        ),
    )
    reduce_start(pay_b, first_b, send_b1, receive_b1, own, plane)
    reduce_middle(*round_b)
    direction_rows = permuted(direction, onehot_ref[...], nt)
    projected_rows = permuted(projected, onehot_ref[...], nt)
    order = (
        iota((NC, NC), 1)
        == MODES * jnp.bitwise_and(iota((NC, NC), 0), AGGS - 1) + lax.shift_right_logical(iota((NC, NC), 0), 6)
    ).astype(F32).astype(BF16)
    exchange_sent(message, landed, send_x, receive_x, own, plane)
    reduce_sent(*round_a)
    reduce_finish(*round_b)

    image_coarse, sums = read_result(result_b)
    renewed = sums[:, 2:3]
    ratio = renewed / inner
    bend = sums[:, 0:1] + ratio * sums[:, 1:2] + ratio * ratio * curvature
    step_next = renewed / bend
    coarse_last = coarse_next - step_next * (image_coarse + ratio * coarse_jump)
    final = nn(coarse_last, inverse_ref[...], HIGHEST)
    amplitudes_ref[...] = permuted(final, order, nn)
    multipliers_ref[...] = (
        step * direction_rows + step_next * (projected_rows + ratio * direction_rows)
    )
    reduce_sent(*round_b)


VMEM = pl.BlockSpec(memory_space=pltpu.VMEM)
DMA = pltpu.SemaphoreType.DMA


def shape(dims, kind=F32):
    return jax.ShapeDtypeStruct(dims, kind)


def body(dual_ops, mode_traces, route, mode_block, local_gap):
    blocks = mode_block.reshape(SUB, REP)
    residual, basis, glued, onehot, gram, coarse, norm = pl.pallas_call(
        setup_kernel,
        out_shape=(
            shape((CASES, ROWS)), shape((NC, ROWS)), shape((ROWS, ROWS), BF16),
            shape((ROWS, ROWS), BF16), shape((NC, NC)), shape((CASES, NC)), shape((CASES, 128)),
        ),
        in_specs=[VMEM] * 5,
        out_specs=(VMEM,) * 7,
        scratch_shapes=[
            pltpu.VMEM((SUB, 8, 128), F32), pltpu.VMEM((SUB, 8, 128), F32),
            pltpu.VMEM((ROWS, ROWS), BF16), pltpu.VMEM((ROWS, ROWS), BF16),
            pltpu.VMEM((2, 128, ROWS), F32), pltpu.VMEM((128, ROWS), F32),
            pltpu.VMEM((SUB, 1, 128), F32), pltpu.VMEM((SUB, 1, 128), F32),
            pltpu.VMEM((SLICE, 128), F32), pltpu.VMEM((REP, SLICE, 128), F32),
            pltpu.VMEM((SLICE, 128), F32), pltpu.VMEM((SUB, SLICE, 128), F32),
            DMA((SUB,)), DMA((SUB,)), DMA((SUB,)), DMA((SUB,)),
            DMA((REP,)), DMA((REP,)), DMA((SUB,)), DMA((SUB,)),
        ],
        compiler_params=pltpu.CompilerParams(
            collective_id=0, has_side_effects=True, vmem_limit_bytes=48 * 1024 * 1024
        ),
        name="setup",
    )(dual_ops, mode_traces, route, blocks, local_gap)
    inverse = pl.pallas_call(
        invert_kernel,
        out_shape=shape((NC, NC)),
        in_specs=[VMEM],
        out_specs=VMEM,
        name="invert",
    )(gram)
    tile = pltpu.VMEM((8, 128), F32)
    many = pltpu.VMEM((SUB, 8, 128), F32)
    few = pltpu.VMEM((TILES, 8, 128), F32)
    return pl.pallas_call(
        solve_kernel,
        out_shape=(shape((CASES, ROWS)), shape((CASES, NC))),
        in_specs=[VMEM] * 7,
        out_specs=(VMEM,) * 2,
        scratch_shapes=[many, many] + [few, many, tile, few, tile, few] * 2
        + [DMA((SUB,)), DMA((SUB,))]
        + [DMA((TILES,)), DMA((SUB,)), DMA((REP,)), DMA((REP,)), DMA((SUB,)), DMA((TILES,))] * 2,
        compiler_params=pltpu.CompilerParams(
            collective_id=1, has_side_effects=True, vmem_limit_bytes=48 * 1024 * 1024
        ),
        name="solve",
    )(residual, basis, glued, onehot, inverse, coarse, norm)


def solution(mesh):
    placed = (
        P(("sub", "rep"), None, None),
        P(("sub", "rep"), None, None),
        P(("sub", "rep"), None),
        P(),
        P(None, ("sub", "rep")),
    )
    return jax.shard_map(
        body, mesh=mesh, in_specs=placed, out_specs=(P(None, ("sub", "rep")), P()), check_vma=False
    )
```

time: 1070 us -> 195 us (0.18)
  blocking collectives: 383 us -> 0 us
  waiting for transfers between devices: 350 us -> 0 us
  Pallas kernels: 0 us -> 183 us
  other arithmetic: 120 us -> 1.35 us
  local copies, waits for them, and re-layouts: 122 us -> 8.63 us
  starting transfers between devices: 40.8 us -> 0 us
  matrix products: 26.6 us -> 0 us
  between operations: 19.1 us -> 0.67 us
    psum x3 -> x0, blocking collectives: 364 us -> none  [the longest x2 234 us: body(): lax.psum((coarse_term(image_jump), jnp.sum(image_jump * image_jump, axis=...]
    psum x1 -> x0, waiting for transfers between devices: 340 us -> none  [body(): lax.psum((gram_term, coarse_term(residual), squares), ('sub', 'rep'))]
    pallas_call x0 -> x3, Pallas kernels: none -> 183 us  [the longest x1 82.3 us: body(): pl.pallas_call(setup_kernel, out_shape=(shape((CASES, ROWS)), shape((NC,...]
    another operation x14 -> x0, other arithmetic: 88.5 us -> none  [the longest x10 56.4 us: body(): factor = jnp.linalg.cholesky(gram_matrix)]
    gather x17 -> x0, local copies, waits for them, and re-layouts: 64.4 us -> none  [the longest x3 14.4 us: to_peers(): return values[:, slot_rows]]
    all_to_all x3 -> x0, starting transfers between devices: 40.8 us -> none  [the longest x1 18.2 us: body(): lax.all_to_all(trace_slots, 'sub', split_axis=1, concat_axis=1, tiled=True)]
    all_to_all x1 -> x0, blocking collectives: 18.9 us -> none  [body(): lax.all_to_all(to_peers(product), 'sub', split_axis=1, concat_axis=1, til...]
    dot_general x11 -> x0, matrix products: 14.1 us -> none  [the longest x3 3.81 us: coarse_term(): own_part = 2.0 * jnp.dot(values, traces.T, precision=HIGHEST)]
  transfers between devices with their start and end apart: 4 -> 0, of which waited for: 2 -> 0; matrix products, arithmetic and copies ran while one was open for 5% -> 0% of each run, Pallas kernels for 0% -> 0%
where the time goes in v1:
time: 195 us; the launch traced here: 194 us
  Pallas kernels  183 us (94%)
  local copies, waits for them, and re-layouts  8.63 us (4%)
    pallas_call x1, Pallas kernels, body(): pl.pallas_call(setup_kernel, out_shape=(shape((CASES, ROWS)), shape((NC,...  82.3 us
    pallas_call x1, Pallas kernels, body(): pl.pallas_call(solve_kernel, out_shape=(shape((CASES, ROWS)), shape((CASE...  62.5 us
    pallas_call x1, Pallas kernels, body(): pl.pallas_call(invert_kernel, out_shape=shape((NC, NC)), in_specs=[VMEM],...  38.4 us
    unnamed x16, local copies, waits for them, and re-layouts  8.56 us

profile of v1, /device:TPU:1, one launch (start us, length us, event | category | flops | bytes accessed | tf_op | source)
XLA Modules:
  0.0 193.8 jit_solution(9405004957917630993)
XLA Ops:
  0.6 0.5 broadcast.3
  1.1 1.3 reduce.3
  2.5 0.1 reshape.7.blocks_ref
  2.6 0.7 copy.8.traces_ref
  3.3 0.0 copy-start.4
  3.3 0.9 copy-done.4
  4.2 0.0 copy-start.5
  4.2 0.7 copy-done.5
  4.9 82.3 %setup.1 = (f32[32,1024]{1,0:T(8,128)S(1)}, f32[384,1024]{1,0:T(8,128)S(1)}, bf16[1024,1024]{1,0:T(8,128)(2,1)S(1)}, bf16[1024,1024]{1,0:T(8,128)(2,1)}, f32[384...) custom-call(bf16[1,1024,1024]{2,1,0:T(8,128)(2,1)} %operator_ref.1, ...), custom_call_target="tpu_custom_call" | custom-call | tf_op jit(solution)/shard_map/setup/pallas_call | solution.py:519
  87.2 0.0 copy-start.1
  87.2 1.1 copy-done.1
  88.3 0.0 copy-start.3
  88.3 0.8 copy-done.3
  89.1 38.4 %invert.1.inverse_ref = f32[384,384]{1,0:T(8,128)} custom-call(f32[384,384]{1,0:T(8,128)} %copy-done.3), custom_call_target="tpu_custom_call" | custom-call | tf_op jit(solution)/shard_map/invert/pallas_call | solution.py:542
  127.5 0.0 copy-start
  127.5 1.1 copy-done
  128.6 0.0 copy-start.2
  128.6 1.4 copy-done.2
  130.0 62.5 %solve.1 = (f32[32,1024]{1,0:T(8,128)S(1)}, f32[32,384]{1,0:T(8,128)S(1)}) custom-call(f32[32,1024]{1,0:T(8,128)S(1)} %get-tuple-element.9.residual_ref, f32[384,1024]{1,0:T(8,128)S(1)} %copy-done.2, bf16[1024,1024]{1,0:T(8,128)(2,1)S(1)} %get-tuple-element.11.glued_ref, bf16[1024,1024]{1,0:T(8,128)(2,1)} %get-tuple-element.12.onehot_ref, ...), custom_call_target="tpu_custom_call" | custom-call | tf_op jit(solution)/shard_map/solve/pallas_call | solution.py:552
  192.6 0.7 copy.11
  193.2 0.6 copy.12
Async XLA Ops:
  3.3 0.9 copy-start.4
  4.2 0.7 copy-start.5
  87.2 1.2 copy-start.1
  88.3 0.8 copy-start.3
  127.5 1.1 copy-start
  128.6 1.4 copy-start.2

commit v2 on v1

--- a/solution.py
+++ b/solution.py
@@ -16,6 +16,7 @@
 TILES = 16
 SLICE = 24
 HALF = 24
+LIMIT = 24 * 1024 * 1024
 F32 = jnp.float32
 BF16 = jnp.bfloat16
 HIGHEST = lax.Precision.HIGHEST
@@ -42,9 +43,18 @@
     return high, middle, low
 
 
+def stacked(values):
+    return jnp.concatenate(split(values), axis=0)
+
+
 def permuted(values, onehot, product):
-    high, middle, low = split(values)
-    return (product(high, onehot) + product(middle, onehot)) + product(low, onehot)
+    rows = values.shape[0]
+    parts = product(stacked(values), onehot)
+    return (parts[:rows] + parts[rows : 2 * rows]) + parts[2 * rows :]
+
+
+def row_sum(values):
+    return jnp.sum(values, axis=1, keepdims=True)
 
 
 def iota(shape, dim):
@@ -178,19 +188,24 @@
     lax.fori_loop(1, REP, one, 0)
 
 
+def block_of(peer):
+    return lax.rem(peer, 8) * 8 + peer // 8
+
+
 def setup_kernel(
     operator_ref, traces_ref, route_ref, blocks_ref, gap_ref,
-    residual_ref, basis_ref, glued_ref, onehot_ref, gram_ref, coarse_ref, norm_ref,
-    message, landed, rows_ref, half_ref, pair_ref, even_ref,
+    residual_ref, modes_ref, mask_ref, own_ref, glued_ref, onehot_ref,
+    gram_ref, coarse_ref, norm_ref,
+    message, landed, rows_ref, half_ref,
     gram_out, gram_in, part_ref, column_in, total_ref, gathered,
-    send_a, receive_a, send_b, receive_b, send_c, receive_c, send_d, receive_d,
+    send_a, receive_a, send_b, receive_b, send_c, receive_c,
+    send_d, receive_d, send_e, receive_e, send_f, receive_f,
 ):
     own = lax.axis_index("sub")
     plane = lax.axis_index("rep")
     barrier = greet(own, plane)
 
     route_row = route_ref[...]
-    wide_route = jnp.broadcast_to(route_row, (128, ROWS)).astype(F32)
 
     @pl.loop(0, 4)
     def _(step):
@@ -198,73 +213,80 @@
         hit = iota((256, ROWS), 0) + step * 256 == route_row
         onehot_ref[rows, :] = hit.astype(F32).astype(BF16)
 
-    stacked = jnp.concatenate(
-        [gap_ref[...], traces_ref[0], jnp.zeros((2, ROWS), F32)], axis=0
-    )
-    ordered = permuted(stacked, onehot_ref[...], nn)
-    pack(jnp.concatenate([ordered, jnp.zeros((24, ROWS), F32)], axis=0), message)
+    natural = jnp.concatenate(
+        [gap_ref[...]] + [traces_ref[k] for k in range(MODES)] + [jnp.zeros((10, ROWS), F32)],
+        axis=0,
+    )
+    ordered = permuted(natural, onehot_ref[...], nn)
+    pack(jnp.concatenate([ordered, jnp.zeros((16, ROWS), F32)], axis=0), message)
 
     pl.semaphore_wait(barrier, SUB - 1 + REP - 1)
     exchange_start(message, landed, send_a, receive_a, own, plane)
     flip_own(message, landed, own)
 
-    tall_route = jnp.transpose(wide_route)
-    for tile in range(8):
-        hit = tall_route == (iota((ROWS, 128), 1) + tile * 128).astype(F32)
-        rows_ref[:, tile * 128 : tile * 128 + 128] = hit.astype(F32).astype(BF16)
+    repeat = (iota((128, ROWS), 1) // PER == iota((128, ROWS), 0)).astype(F32).astype(BF16)
+    blocks = jnp.where(
+        lax.rem(iota((1, ROWS), 1), REP) == plane, blocks_ref[...].astype(F32), 0.0
+    )
+    peer_block = nt(jnp.broadcast_to(blocks, (16, ROWS)).astype(BF16), repeat)[:1]
+    hit = jnp.logical_and(
+        peer_block == iota((128, 128), 0).astype(F32), iota((128, 128), 1) < SUB
+    )
+    by_block = hit.astype(F32)
+    by_peer = jnp.transpose(by_block)
+    mask = nn(by_block.astype(BF16), repeat).astype(BF16)
+    mask_ref[...] = mask
+    own_row = jnp.sum(
+        jnp.where(iota((128, 128), 0) == own, by_peer, 0.0), axis=0, keepdims=True
+    )
+    own_ref[...] = jnp.broadcast_to(own_row, (8, 128))
+    traces = ordered[CASES : CASES + 8]
+    modes_ref[0] = traces
+    own_part = jnp.concatenate(
+        [row_sum(traces * traces[k : k + 1]) for k in range(MODES)], axis=0
+    )
 
     @pl.loop(0, 4)
     def _(step):
         rows = pl.ds(pl.multiple_of(step * 256, 256), 256)
         half_ref[rows, :] = nn(operator_ref[0, rows, :], onehot_ref[...]).astype(BF16)
 
-    @pl.loop(0, 4)
-    def _(step):
-        rows = pl.ds(pl.multiple_of(step * 256, 256), 256)
-        glued_ref[rows, :] = nn(rows_ref[rows, :], half_ref[...]).astype(BF16)
-
-    blocks = blocks_ref[...].astype(F32)
-    picked = jnp.where(iota((SUB, REP), 1) == plane, blocks, 0.0)
-    peer_block = jnp.sum(picked, axis=1, keepdims=True)
-    hit = peer_block == iota((SUB, 128), 1).astype(F32)
-    by_peer = jnp.concatenate([hit.astype(F32), jnp.zeros((64, 128), F32)], axis=0)
-    by_block = jnp.transpose(by_peer)
-    repeat = (iota((128, ROWS), 1) // PER == iota((128, ROWS), 0)).astype(F32).astype(BF16)
-    peer_mask = nn(by_block[:AGGS].astype(BF16), repeat)
-    own_mask = jnp.sum(
-        jnp.where(iota((AGGS, 128), 1) == own, by_block[:AGGS], 0.0), axis=1, keepdims=True
-    )
-    traces = ordered[CASES : CASES + 8]
-    pair_ref[...] = jnp.zeros_like(pair_ref)
-    even_ref[...] = jnp.zeros_like(even_ref)
-    for k in range(MODES):
-        row = traces[k : k + 1]
-        at = k // 2 + HALF * (k % 2)
-        even_ref[at : at + 1, :] = row
-        lane = (18, 42, 19)[k // 2]
-        pair_ref[k % 2, lane : lane + 1, :] = row
-
     exchange_wait(message, landed, send_a, receive_a, own, plane)
     partner = unpack(landed)
     residual = ordered[:CASES] - partner[:CASES]
     residual_ref[...] = residual
-    for k in range(MODES):
-        basis_ref[64 * k : 64 * k + 64, :] = (
-            own_mask * traces[k : k + 1] - peer_mask * partner[CASES + k : CASES + k + 1]
-        )
-    crossed = 2.0 * nt(basis_ref[...], even_ref[...], HIGHEST)
-    outgoing = crossed[:64]
-    for k in range(1, MODES):
-        outgoing = outgoing + pltpu.roll(crossed[64 * k : 64 * k + 64], 3 * k, 1)
-    first = 2.0 * nt(residual, pair_ref[0], HIGHEST)
-    second = 2.0 * nt(residual, pair_ref[1], HIGHEST)
-    squares = jnp.sum(residual * residual, axis=1, keepdims=True)
-    first = jnp.where(iota((CASES, 128), 1) == 43, squares, first)
-    gram_out[...] = (outgoing + jnp.concatenate([first, second], axis=0)).reshape(SUB, 1, 128)
-
-    exchange_start(gram_out, gram_in, send_b, receive_b, own, plane)
-    gram_in[own] = gram_out[own]
-    exchange_sent(message, landed, send_a, receive_a, own, plane)
+    far = partner[CASES : CASES + 8]
+    modes_ref[1] = far
+    pairs = jnp.concatenate([traces * far[k : k + 1] for k in range(MODES)], axis=0)
+    crossed = 2.0 * (own_part * own_row - permuted(pairs, mask, nt))
+    upright = jnp.transpose(jnp.concatenate([crossed, jnp.zeros((80, 128), F32)], axis=0))
+    terms = [2.0 * row_sum(residual * traces[k : k + 1]) for k in range(MODES)]
+    squares = row_sum(residual * residual)
+    outgoing = upright[:AGGS]
+    lane = iota((AGGS, 128), 1)
+    for at, (upper, lower) in (
+        (6, (terms[0], terms[1])),
+        (30, (terms[2], terms[3])),
+        (7, (terms[4], terms[5])),
+        (31, (squares, jnp.zeros_like(squares))),
+    ):
+        outgoing = jnp.where(lane == at, jnp.concatenate([upper, lower], axis=0), outgoing)
+    gram_out[...] = outgoing.reshape(AGGS, 1, 128)
+
+    def give(i, _):
+        peer = lax.rem(own + i, SUB)
+        to_peer(
+            gram_out.at[block_of(peer)], gram_in.at[own], send_b.at[peer], receive_b.at[own],
+            peer, plane,
+        ).start()
+        return 0
+
+    lax.fori_loop(1, SUB, give, 0)
+    gram_in[own] = gram_out[block_of(own)]
+    tall_route = jnp.transpose(jnp.broadcast_to(route_row, (128, ROWS)).astype(F32))
+    for tile in range(8):
+        hit = tall_route == (iota((ROWS, 128), 1) + tile * 128).astype(F32)
+        rows_ref[:, tile * 128 : tile * 128 + 128] = hit.astype(F32).astype(BF16)
     exchange_wait(gram_out, gram_in, send_b, receive_b, own, plane)
     arrived = gram_in[...].reshape(SUB, 128)
     turned = jnp.transpose(jnp.concatenate([arrived, jnp.zeros((64, 128), F32)], axis=0))
@@ -273,53 +295,200 @@
 
     column(part_ref, column_in, send_c, receive_c, own, plane, "start")
     column_in[plane] = part_ref[...]
-    exchange_sent(gram_out, gram_in, send_b, receive_b, own, plane)
+
+    @pl.loop(0, 4)
+    def _(step):
+        rows = pl.ds(pl.multiple_of(step * 256, 256), 256)
+        glued_ref[rows, :] = nn(rows_ref[rows, :], half_ref[...]).astype(BF16)
+
     column(part_ref, column_in, send_c, receive_c, own, plane, "recv")
     total_ref[...] = jnp.sum(column_in[...], axis=0)
 
-    spread_start(total_ref, gathered, own, send_d, receive_d, own, plane)
-    gathered[own] = total_ref[...]
-    column(part_ref, column_in, send_c, receive_c, own, plane, "sent")
-    exchange_wait(gathered, gathered, send_d, receive_d, own, plane)
-    for k in range(MODES):
+    line = own // 8
+    group = lax.rem(own, 8)
+    across = group // 2
+    core = lax.rem(own, 2)
+
+    def along_y(i, act):
+        other = lax.rem(line + i, 8)
+        index = group * 8 + (line if act == "start" else other)
+        copy = to_peer(
+            total_ref, gathered.at[index], send_d.at[other],
+            receive_d.at[line if act == "start" else other], other * 8 + group, plane,
+        )
+        return copy
+
+    def along_x(i, act):
+        other = lax.rem(across + i, 4)
+        source = gathered.at[pl.ds(8 * group, 8)]
+        index = across if act == "start" else other
+        return to_peer(
+            source, gathered.at[pl.ds(8 * (2 * index + core), 8)], send_e.at[other],
+            receive_e.at[index], line * 8 + 2 * other + core, plane,
+        )
+
+    def to_sibling(other, act):
+        index = 2 * other + (core if act == "start" else 1 - core)
+        return to_peer(
+            gathered.at[pl.ds(8 * (2 * other + core), 8)], gathered.at[pl.ds(8 * index, 8)],
+            send_f.at[other], receive_f.at[other], line * 8 + 2 * across + 1 - core, plane,
+        )
+
+    for i in range(1, 8):
+        along_y(i, "start").start()
+    gathered[block_of(own)] = total_ref[...]
+    for i in range(1, 8):
+        along_y(i, "recv").wait_recv()
+    for i in range(1, 4):
+        along_x(i, "start").start()
+    to_sibling(across, "start").start()
+    for i in (1, 3, 2):
+        along_x(i, "recv").wait_recv()
+        to_sibling(lax.rem(across + i, 4), "start").start()
+    for i in range(4):
+        to_sibling(i, "recv").wait_recv()
+
+    low = iota((AGGS, 128), 1) < 64
+    for k in range(3):
         for j in range(3):
-            gram_ref[64 * k : 64 * k + 64, 128 * j : 128 * j + 128] = gathered[:, 3 * k + j, :]
-    near = gathered[:, 18, :]
-    far = gathered[:, 19, :]
-    even_odd = (near, pltpu.roll(near, 64, 1), far)
-    lower = iota((CASES, 128), 1) < 64
+            even = gathered[:, 8 * k + 2 * j, :]
+            odd = gathered[:, 8 * k + 2 * j + 1, :]
+            columns = pl.ds(128 * j, 128)
+            gram_ref[64 * k : 64 * k + 64, columns] = jnp.where(low, even, pltpu.roll(odd, 64, 1))
+            gram_ref[64 * k + 192 : 64 * k + 256, columns] = jnp.where(
+                low, pltpu.roll(even, 64, 1), odd
+            )
+    near = gathered[:, 6, :]
+    last = gathered[:, 7, :]
+    folded = (near, pltpu.roll(near, 64, 1), last)
     for i in range(3):
         coarse_ref[:, 128 * i : 128 * i + 128] = jnp.where(
-            lower, even_odd[i][:CASES], pltpu.roll(even_odd[i][CASES:], 64, 1)
+            low[:CASES], folded[i][:CASES], pltpu.roll(folded[i][CASES:], 64, 1)
         )
-    totals = jnp.sum(jnp.where(iota((CASES, 128), 1) >= 64, far[:CASES], 0.0), axis=1, keepdims=True)
-    norm_ref[...] = jnp.broadcast_to(totals, (CASES, 128))
-    spread_sent(total_ref, gathered, own, send_d, receive_d, own, plane)
-
-
-def invert_kernel(gram_ref, inverse_ref):
-    inverse_ref[...] = gram_ref[...]
-    lane = iota((128, 128), 1)
-    line = iota((128, 128), 0)
+    norm_ref[...] = jnp.broadcast_to(
+        row_sum(jnp.where(low[:CASES], 0.0, last[:CASES])), (CASES, 128)
+    )
+    exchange_sent(message, landed, send_a, receive_a, own, plane)
+    exchange_sent(gram_out, gram_in, send_b, receive_b, own, plane)
+    column(part_ref, column_in, send_c, receive_c, own, plane, "sent")
+    for i in range(1, 8):
+        along_y(i, "start").wait_send()
+    for i in range(1, 4):
+        along_x(i, "start").wait_send()
+    for i in range(4):
+        to_sibling(i, "start").wait_send()
+
+
+def invert_block(pivot):
+    tiles = pivot.reshape(16, 8, 128)
+    lane = iota((8, 128), 1)
+    line = iota((8, 128), 0)
+    for k in range(0, 128, 4):
+        tile, at = k // 8, k % 8
+        lefts = [
+            jnp.broadcast_to(tiles[:, :, k + m : k + m + 1], (16, 8, 128)) for m in range(4)
+        ]
+        rows = [
+            jnp.broadcast_to(tiles[tile, at + m : at + m + 1, :], (8, 128)) for m in range(4)
+        ]
+        small = [
+            [jnp.broadcast_to(lefts[n][tile, at + m : at + m + 1, :], (8, 128)) for n in range(4)]
+            for m in range(4)
+        ]
+        for p in range(4):
+            scale = 1.0 / small[p][p]
+            pivots = [scale if n == p else small[p][n] * scale for n in range(4)]
+            for m in range(4):
+                if m != p:
+                    factor = small[m][p]
+                    small[m] = [
+                        -factor * scale if n == p else small[m][n] - factor * pivots[n]
+                        for n in range(4)
+                    ]
+            small[p] = pivots
+        fresh = []
+        for m in range(4):
+            row = (small[m][0] * rows[0] + small[m][1] * rows[1]) + (
+                small[m][2] * rows[2] + small[m][3] * rows[3]
+            )
+            for n in range(4):
+                row = jnp.where(lane == k + n, small[m][n], row)
+            fresh.append(row)
+        inside = jnp.logical_and(lane >= k, lane < k + 4)
+        kept = jnp.where(inside[None], 0.0, tiles)
+        moved = kept - (
+            (lefts[0] * fresh[0][None] + lefts[1] * fresh[1][None])
+            + (lefts[2] * fresh[2][None] + lefts[3] * fresh[3][None])
+        )
+        own = moved[tile]
+        for m in range(4):
+            own = jnp.where(line == at + m, fresh[m], own)
+        pieces = [own[None]]
+        if tile > 0:
+            pieces.insert(0, moved[:tile])
+        if tile < 15:
+            pieces.append(moved[tile + 1 :])
+        tiles = jnp.concatenate(pieces, axis=0)
+    return tiles.reshape(128, 128)
+
+
+def invert_kernel(gram_ref, coarse_ref, parts_ref, start_ref, work):
+    work[...] = gram_ref[...]
 
     @pl.loop(0, 3)
     def _(block):
         at = pl.ds(pl.multiple_of(block * 128, 128), 128)
-        pivot = inverse_ref[at, at]
-        for k in range(128):
-            scale = 1.0 / pivot[k : k + 1, k : k + 1]
-            row = jnp.where(lane[:1] == k, scale, pivot[k : k + 1, :] * scale)
-            left = pivot[:, k : k + 1]
-            kept = jnp.where(lane == k, 0.0, pivot)
-            pivot = jnp.where(line == k, row, kept - left * row)
-        rows = nn(pivot, inverse_ref[at, :], HIGHEST)
-        lefts = inverse_ref[:, at]
+        pivot = invert_block(work[at, at])
+        rows = nn(pivot, work[at, :], HIGHEST)
         mine = iota((NC, 128), 0) // 128 == block
-        lefts = jnp.where(mine, 0.0, lefts)
-        inverse_ref[...] = inverse_ref[...] - nn(lefts, rows, HIGHEST)
-        inverse_ref[:, at] = -nn(lefts, pivot, HIGHEST)
-        inverse_ref[at, :] = rows
-        inverse_ref[at, at] = pivot
+        lefts = jnp.where(mine, 0.0, work[:, at])
+        work[...] = work[...] - nn(lefts, rows, HIGHEST)
+        work[:, at] = -nn(lefts, pivot, HIGHEST)
+        work[at, :] = rows
+        work[at, at] = pivot
+
+    high, middle, low = split(work[...])
+    parts_ref[0] = high
+    parts_ref[1] = middle
+    parts_ref[2] = low
+    start_ref[...] = solved(coarse_ref[...], parts_ref)
+
+
+def solved(right, parts_ref):
+    high, middle, low = split(right)
+    one = nn(jnp.concatenate([high, middle, low], axis=0), parts_ref[0])
+    two = nn(jnp.concatenate([high, middle], axis=0), parts_ref[1])
+    three = nn(high, parts_ref[2])
+    small = (one[2 * CASES :] + two[CASES:]) + three
+    return one[:CASES] + ((one[CASES : 2 * CASES] + two[:CASES]) + small)
+
+
+def coarse_terms(values, modes_ref, mask, own_row):
+    far = jnp.concatenate([values * modes_ref[1, k : k + 1] for k in range(MODES)], axis=0)
+    spread = permuted(far, mask, nt)
+    columns = []
+    for k in range(MODES):
+        near = row_sum(values * modes_ref[0, k : k + 1])
+        columns.append(2.0 * (near * own_row - spread[CASES * k : CASES * k + CASES]))
+    return jnp.concatenate(
+        [columns[2 * i] + pltpu.roll(columns[2 * i + 1], 64, 1) for i in range(3)], axis=1
+    )
+
+
+def expand(amounts, modes_ref, mask, own_row):
+    low = iota((CASES, 128), 1) < 64
+    pieces = []
+    for i in range(3):
+        both = amounts[:, 128 * i : 128 * i + 128]
+        pieces.append(jnp.where(low, both, 0.0))
+        pieces.append(jnp.where(low, pltpu.roll(both, 64, 1), 0.0))
+    spread = permuted(jnp.concatenate(pieces, axis=0), mask, nn)
+    total = None
+    for k in range(MODES):
+        near = row_sum(pieces[k] * own_row)
+        term = near * modes_ref[0, k : k + 1] - spread[CASES * k : CASES * k + CASES] * modes_ref[1, k : k + 1]
+        total = term if total is None else total + term
+    return total
 
 
 def owner_of(tile):
@@ -423,12 +592,9 @@
     return jnp.concatenate(columns[:3], axis=1), columns[3]
 
 
-def row_sum(values):
-    return jnp.sum(values, axis=1, keepdims=True)
-
-
 def solve_kernel(
-    residual_ref, basis_ref, glued_ref, onehot_ref, inverse_ref, coarse_ref, norm_ref,
+    residual_ref, modes_ref, mask_ref, own_ref, glued_ref, onehot_ref,
+    parts_ref, start_ref, coarse_ref, norm_ref,
     multipliers_ref, amplitudes_ref,
     message, landed, pay_a, first_a, mid_a, second_a, last_a, result_a,
     pay_b, first_b, mid_b, second_b, last_b, result_b,
@@ -446,12 +612,18 @@
 
     residual = residual_ref[...]
     coarse = coarse_ref[...]
-    start = nn(coarse, inverse_ref[...], HIGHEST)
-    direction = residual - nn(start, basis_ref[...], HIGHEST)
+    start = start_ref[...]
+    mask = mask_ref[...]
+    own_row = own_ref[:1]
+    direction = residual - expand(start, modes_ref, mask, own_row)
     inner = norm_ref[:, :1] - row_sum(start * coarse)
     product = nt(direction.astype(BF16), glued_ref[...])
     pack(jnp.concatenate([product, jnp.zeros((32, ROWS), F32)], axis=0), message)
-    load_pay(pay_a, 2.0 * nt(product, basis_ref[...], HIGHEST), (2.0 * row_sum(direction * product),))
+    load_pay(
+        pay_a,
+        coarse_terms(product, modes_ref, mask, own_row),
+        (2.0 * row_sum(direction * product),),
+    )
 
     pl.semaphore_wait(barrier, SUB - 1 + REP - 1)
     reduce_start(pay_a, first_a, send_a1, receive_a1, own, plane)
@@ -466,14 +638,16 @@
     curvature = sums[:, 0:1]
     step = inner / curvature
     coarse_next = coarse - step * coarse_jump
-    amplitudes = nn(coarse_next, inverse_ref[...], HIGHEST)
-    projected = (residual - step * jumped) - nn(amplitudes, basis_ref[...], HIGHEST)
+    amplitudes = solved(coarse_next, parts_ref)
+    projected = (residual - step * jumped) - expand(
+        amplitudes, modes_ref, mask, own_row
+    )
     high, low, _ = split(projected)
     both = nt(jnp.concatenate([high, low], axis=0), glued_ref[...])
     image = both[:CASES] + both[CASES:]
     load_pay(
         pay_b,
-        2.0 * nt(image, basis_ref[...], HIGHEST),
+        coarse_terms(image, modes_ref, mask, own_row),
         (
             2.0 * row_sum(projected * image),
             2.0 * row_sum(projected * product) + 2.0 * row_sum(direction * image),
@@ -498,7 +672,7 @@
     bend = sums[:, 0:1] + ratio * sums[:, 1:2] + ratio * ratio * curvature
     step_next = renewed / bend
     coarse_last = coarse_next - step_next * (image_coarse + ratio * coarse_jump)
-    final = nn(coarse_last, inverse_ref[...], HIGHEST)
+    final = solved(coarse_last, parts_ref)
     amplitudes_ref[...] = permuted(final, order, nn)
     multipliers_ref[...] = (
         step * direction_rows + step_next * (projected_rows + ratio * direction_rows)
@@ -515,53 +689,61 @@
 
 
 def body(dual_ops, mode_traces, route, mode_block, local_gap):
-    blocks = mode_block.reshape(SUB, REP)
-    residual, basis, glued, onehot, gram, coarse, norm = pl.pallas_call(
+    residual, modes, mask, own, glued, onehot, gram, coarse, norm = pl.pallas_call(
         setup_kernel,
         out_shape=(
-            shape((CASES, ROWS)), shape((NC, ROWS)), shape((ROWS, ROWS), BF16),
-            shape((ROWS, ROWS), BF16), shape((NC, NC)), shape((CASES, NC)), shape((CASES, 128)),
+            shape((CASES, ROWS)), shape((2, 8, ROWS)), shape((128, ROWS), BF16), shape((8, 128)),
+            shape((ROWS, ROWS), BF16), shape((ROWS, ROWS), BF16),
+            shape((NC, NC)), shape((CASES, NC)), shape((CASES, 128)),
         ),
         in_specs=[VMEM] * 5,
-        out_specs=(VMEM,) * 7,
+        out_specs=(VMEM,) * 9,
         scratch_shapes=[
             pltpu.VMEM((SUB, 8, 128), F32), pltpu.VMEM((SUB, 8, 128), F32),
             pltpu.VMEM((ROWS, ROWS), BF16), pltpu.VMEM((ROWS, ROWS), BF16),
-            pltpu.VMEM((2, 128, ROWS), F32), pltpu.VMEM((128, ROWS), F32),
-            pltpu.VMEM((SUB, 1, 128), F32), pltpu.VMEM((SUB, 1, 128), F32),
+            pltpu.VMEM((AGGS, 1, 128), F32), pltpu.VMEM((SUB, 1, 128), F32),
             pltpu.VMEM((SLICE, 128), F32), pltpu.VMEM((REP, SLICE, 128), F32),
-            pltpu.VMEM((SLICE, 128), F32), pltpu.VMEM((SUB, SLICE, 128), F32),
+            pltpu.VMEM((SLICE, 128), F32), pltpu.VMEM((AGGS, SLICE, 128), F32),
             DMA((SUB,)), DMA((SUB,)), DMA((SUB,)), DMA((SUB,)),
-            DMA((REP,)), DMA((REP,)), DMA((SUB,)), DMA((SUB,)),
+            DMA((REP,)), DMA((REP,)), DMA((8,)), DMA((8,)),
+            DMA((4,)), DMA((4,)), DMA((4,)), DMA((4,)),
         ],
         compiler_params=pltpu.CompilerParams(
-            collective_id=0, has_side_effects=True, vmem_limit_bytes=48 * 1024 * 1024
+            collective_id=0, has_side_effects=True, vmem_limit_bytes=LIMIT
         ),
         name="setup",
-    )(dual_ops, mode_traces, route, blocks, local_gap)
-    inverse = pl.pallas_call(
+    )(
+        dual_ops,
+        jnp.transpose(mode_traces, (1, 0, 2)),
+        route,
+        mode_block.reshape(1, SUB * REP),
+        local_gap,
+    )
+    parts, start = pl.pallas_call(
         invert_kernel,
-        out_shape=shape((NC, NC)),
-        in_specs=[VMEM],
-        out_specs=VMEM,
+        out_shape=(shape((3, NC, NC), BF16), shape((CASES, NC))),
+        in_specs=[VMEM] * 2,
+        out_specs=(VMEM,) * 2,
+        scratch_shapes=[pltpu.VMEM((NC, NC), F32)],
+        compiler_params=pltpu.CompilerParams(vmem_limit_bytes=LIMIT),
         name="invert",
-    )(gram)
+    )(gram, coarse)
     tile = pltpu.VMEM((8, 128), F32)
     many = pltpu.VMEM((SUB, 8, 128), F32)
     few = pltpu.VMEM((TILES, 8, 128), F32)
     return pl.pallas_call(
         solve_kernel,
         out_shape=(shape((CASES, ROWS)), shape((CASES, NC))),
-        in_specs=[VMEM] * 7,
+        in_specs=[VMEM] * 10,
         out_specs=(VMEM,) * 2,
         scratch_shapes=[many, many] + [few, many, tile, few, tile, few] * 2
         + [DMA((SUB,)), DMA((SUB,))]
         + [DMA((TILES,)), DMA((SUB,)), DMA((REP,)), DMA((REP,)), DMA((SUB,)), DMA((TILES,))] * 2,
         compiler_params=pltpu.CompilerParams(
-            collective_id=1, has_side_effects=True, vmem_limit_bytes=48 * 1024 * 1024
+            collective_id=1, has_side_effects=True, vmem_limit_bytes=LIMIT
         ),
         name="solve",
-    )(residual, basis, glued, onehot, inverse, coarse, norm)
+    )(residual, modes, mask, own, glued, onehot, parts, start, coarse, norm)
 
 
 def solution(mesh):

time: 195 us -> 166 us (0.85)
  Pallas kernels: 183 us -> 159 us
  local copies, waits for them, and re-layouts: 8.63 us -> 5.87 us
    pallas_call x2, Pallas kernels: 121 us -> 99.7 us  [the longest x1 70.2 us: body(): pl.pallas_call(setup_kernel, out_shape=(shape((CASES, ROWS)), shape((2, 8...]
    pallas_call x1, Pallas kernels: 62.5 us -> 59 us  [body(): pl.pallas_call(solve_kernel, out_shape=(shape((CASES, ROWS)), shape((CASE...]
    unnamed x16 -> x12, local copies, waits for them, and re-layouts: 8.56 us -> 5.87 us
where the time goes in v2:
time: 166 us; the launch traced here: 165 us
  Pallas kernels  159 us (96%)
  local copies, waits for them, and re-layouts  5.87 us (4%)
    pallas_call x1, Pallas kernels, body(): pl.pallas_call(setup_kernel, out_shape=(shape((CASES, ROWS)), shape((2, 8...  70.2 us
    pallas_call x1, Pallas kernels, body(): pl.pallas_call(solve_kernel, out_shape=(shape((CASES, ROWS)), shape((CASE...  59 us
    pallas_call x1, Pallas kernels, body(): pl.pallas_call(invert_kernel, out_shape=(shape((3, NC, NC), BF16), shape(...  29.5 us
    unnamed x12, local copies, waits for them, and re-layouts  5.87 us

profile of v2, /device:TPU:1, one launch (start us, length us, event | category | flops | bytes accessed | tf_op | source)
XLA Modules:
  0.0 165.2 jit_solution(8955397724558158008)
XLA Ops:
  0.6 0.0 copy-start
  0.6 1.6 copy-done
  2.2 0.0 copy-start.1
  2.2 0.9 copy-done.1
  3.1 0.0 copy-start.2
  3.1 0.7 copy-done.2
  3.9 0.0 copy-start.3
  3.9 0.7 copy-done.3
  4.6 0.0 copy-start.4
  4.6 0.7 copy-done.4
  5.2 70.2 %setup.1 = (f32[32,1024]{1,0:T(8,128)S(1)}, f32[2,8,1024]{2,1,0:T(8,128)S(1)}, bf16[128,1024]{1,0:T(8,128)(2,1)S(1)}, f32[8,128]{1,0:T(8,128)S(1)}, bf16[1024,10...) custom-call(bf16[1,1024,1024]{2,1,0:T(8,128)(2,1)S(1)} %copy-done, ...), custom_call_target="tpu_custom_call" | custom-call | tf_op jit(solution)/shard_map/setup/pallas_call | solution.py:692
  75.4 29.5 %invert.1 = (bf16[3,384,384]{2,1,0:T(8,128)(2,1)S(1)}, f32[32,384]{1,0:T(8,128)S(1)}) custom-call(f32[384,384]{1,0:T(8,128)S(1)} %get-tuple-element.19.gram_ref, f32[32,384]{1,0:T(8,128)S(1)} %get-tuple-element.20.coarse_ref), custom_call_target="tpu_custom_call" | custom-call | tf_op jit(solution)/shard_map/invert/pallas_call | solution.py:722
  104.9 59.0 %solve.1 = (f32[32,1024]{1,0:T(8,128)S(1)}, f32[32,384]{1,0:T(8,128)S(1)}) custom-call(f32[32,1024]{1,0:T(8,128)S(1)} %get-tuple-element.13.residual_ref, f32[2,8,1024]{2,1,0:T(8,128)S(1)} %get-tuple-element.14.modes_ref, bf16[128,1024]{1,0:T(8,128)(2,1)S(1)} %get-tuple-element.15.mask_ref, f32[8,128]{1,0:T(8,128)S(1)} %get-tuple-element.16.own_ref, ...), custom_call_target="tpu_custom_call" | custom-call | tf_op jit(solution)/shard_map/solve/pallas_call | solution.py:734
  163.9 0.7 copy.9
  164.5 0.6 copy.10
Async XLA Ops:
  0.6 1.6 copy-start
  2.2 0.9 copy-start.1
  3.1 0.7 copy-start.2
  3.9 0.7 copy-start.3
  4.6 0.7 copy-start.4

commit v3 on v2

--- a/solution.py
+++ b/solution.py
@@ -61,23 +61,39 @@
     return lax.broadcasted_iota(jnp.int32, shape, dim)
 
 
+def each_peer(act):
+    def some(step, _):
+        for j in range(7):
+            act(lax.rem(step * 7 + (j + 23), SUB - 1) + 1)
+        return 0
+
+    lax.fori_loop(0, 9, some, 0)
+
+
+def each_plane(act):
+    def some(step, _):
+        for j in range(5):
+            act(lax.rem(step * 5 + (j + 5), REP - 1) + 1)
+        return 0
+
+    lax.fori_loop(0, 3, some, 0)
+
+
 def greet(own, plane):
     barrier = pltpu.get_barrier_semaphore()
 
-    def over_sub(i, _):
+    def over_sub(i):
         pl.semaphore_signal(
             barrier, inc=1, device_id=(lax.rem(own + i, SUB), plane), device_id_type=MESH
         )
-        return 0
-
-    def over_rep(i, _):
+
+    def over_rep(i):
         pl.semaphore_signal(
             barrier, inc=1, device_id=(own, lax.rem(plane + i, REP)), device_id_type=MESH
         )
-        return 0
-
-    lax.fori_loop(1, SUB, over_sub, 0)
-    lax.fori_loop(1, REP, over_rep, 0)
+
+    each_plane(over_rep)
+    each_peer(over_sub)
     return barrier
 
 
@@ -114,62 +130,57 @@
 
 
 def exchange_start(message_ref, landed_ref, send, receive, own, plane):
-    def one(i, _):
+    def one(i):
         peer = lax.rem(own + i, SUB)
         to_peer(
             message_ref.at[peer], landed_ref.at[own], send.at[peer], receive.at[own], peer, plane
         ).start()
-        return 0
-
-    lax.fori_loop(1, SUB, one, 0)
+
+    each_peer(one)
 
 
 def exchange_wait(message_ref, landed_ref, send, receive, own, plane):
-    def one(i, _):
+    def one(i):
         peer = lax.rem(own + i, SUB)
         to_peer(
             message_ref.at[peer], landed_ref.at[peer], send.at[peer], receive.at[peer], peer, plane
         ).wait_recv()
-        return 0
-
-    lax.fori_loop(1, SUB, one, 0)
+
+    each_peer(one)
 
 
 def exchange_sent(message_ref, landed_ref, send, receive, own, plane):
-    def one(i, _):
+    def one(i):
         peer = lax.rem(own + i, SUB)
         to_peer(
             message_ref.at[peer], landed_ref.at[peer], send.at[peer], receive.at[peer], peer, plane
         ).wait_send()
-        return 0
-
-    lax.fori_loop(1, SUB, one, 0)
+
+    each_peer(one)
 
 
 def spread_start(piece_ref, landed_ref, index, send, receive, own, plane):
-    def one(i, _):
+    def one(i):
         peer = lax.rem(own + i, SUB)
         to_peer(
             piece_ref, landed_ref.at[index], send.at[peer], receive.at[index], peer, plane
         ).start()
-        return 0
-
-    lax.fori_loop(1, SUB, one, 0)
+
+    each_peer(one)
 
 
 def spread_sent(piece_ref, landed_ref, index, send, receive, own, plane):
-    def one(i, _):
+    def one(i):
         peer = lax.rem(own + i, SUB)
         to_peer(
             piece_ref, landed_ref.at[index], send.at[peer], receive.at[index], peer, plane
         ).wait_send()
-        return 0
-
-    lax.fori_loop(1, SUB, one, 0)
+
+    each_peer(one)
 
 
 def column(piece_ref, landed_ref, send, receive, own, plane, act):
-    def one(i, _):
+    def one(i):
         other = lax.rem(plane + i, REP)
         if act == "start":
             to_peer(
@@ -183,9 +194,8 @@
             to_peer(
                 piece_ref, landed_ref.at[other], send.at[other], receive.at[other], own, other
             ).wait_send()
-        return 0
-
-    lax.fori_loop(1, REP, one, 0)
+
+    each_plane(one)
 
 
 def block_of(peer):
@@ -193,18 +203,29 @@
 
 
 def setup_kernel(
-    operator_ref, traces_ref, route_ref, blocks_ref, gap_ref,
+    operator_in, traces_in, route_in, blocks_in, gap_in,
     residual_ref, modes_ref, mask_ref, own_ref, glued_ref, onehot_ref,
     gram_ref, coarse_ref, norm_ref,
     message, landed, rows_ref, half_ref,
     gram_out, gram_in, part_ref, column_in, total_ref, gathered,
     send_a, receive_a, send_b, receive_b, send_c, receive_c,
     send_d, receive_d, send_e, receive_e, send_f, receive_f,
+    operator_ref, traces_ref, route_ref, blocks_ref, gap_ref, loaded,
 ):
+    loads = [
+        pltpu.make_async_copy(source, target, loaded.at[at])
+        for at, (source, target) in enumerate((
+            (route_in, route_ref), (gap_in, gap_ref), (traces_in, traces_ref),
+            (blocks_in, blocks_ref), (operator_in, operator_ref),
+        ))
+    ]
+    for load in loads:
+        load.start()
     own = lax.axis_index("sub")
     plane = lax.axis_index("rep")
     barrier = greet(own, plane)
 
+    loads[0].wait()
     route_row = route_ref[...]
 
     @pl.loop(0, 4)
@@ -213,6 +234,8 @@
         hit = iota((256, ROWS), 0) + step * 256 == route_row
         onehot_ref[rows, :] = hit.astype(F32).astype(BF16)
 
+    loads[1].wait()
+    loads[2].wait()
     natural = jnp.concatenate(
         [gap_ref[...]] + [traces_ref[k] for k in range(MODES)] + [jnp.zeros((10, ROWS), F32)],
         axis=0,
@@ -224,6 +247,8 @@
     exchange_start(message, landed, send_a, receive_a, own, plane)
     flip_own(message, landed, own)
 
+    loads[3].wait()
+    loads[4].wait()
     repeat = (iota((128, ROWS), 1) // PER == iota((128, ROWS), 0)).astype(F32).astype(BF16)
     blocks = jnp.where(
         lax.rem(iota((1, ROWS), 1), REP) == plane, blocks_ref[...].astype(F32), 0.0
@@ -273,15 +298,14 @@
         outgoing = jnp.where(lane == at, jnp.concatenate([upper, lower], axis=0), outgoing)
     gram_out[...] = outgoing.reshape(AGGS, 1, 128)
 
-    def give(i, _):
+    def give(i):
         peer = lax.rem(own + i, SUB)
         to_peer(
             gram_out.at[block_of(peer)], gram_in.at[own], send_b.at[peer], receive_b.at[own],
             peer, plane,
         ).start()
-        return 0
-
-    lax.fori_loop(1, SUB, give, 0)
+
+    each_peer(give)
     gram_in[own] = gram_out[block_of(own)]
     tall_route = jnp.transpose(jnp.broadcast_to(route_row, (128, ROWS)).astype(F32))
     for tile in range(8):
@@ -377,6 +401,15 @@
         along_x(i, "start").wait_send()
     for i in range(4):
         to_sibling(i, "start").wait_send()
+
+
+def swapped(tiles, index, new):
+    pieces = [new[None]]
+    if index > 0:
+        pieces.insert(0, tiles[:index])
+    if index + 1 < tiles.shape[0]:
+        pieces.append(tiles[index + 1 :])
+    return jnp.concatenate(pieces, axis=0)
 
 
 def invert_block(pivot):
@@ -406,33 +439,33 @@
                         for n in range(4)
                     ]
             small[p] = pivots
-        fresh = []
-        for m in range(4):
-            row = (small[m][0] * rows[0] + small[m][1] * rows[1]) + (
-                small[m][2] * rows[2] + small[m][3] * rows[3]
+        inside = jnp.logical_and(lane >= k, lane < k + 4)
+        ready = [
+            jnp.where(inside, jnp.where(lane == k + m, 1.0, 0.0), rows[m]) for m in range(4)
+        ]
+        fresh = [
+            (small[m][0] * ready[0] + small[m][1] * ready[1])
+            + (small[m][2] * ready[2] + small[m][3] * ready[3])
+            for m in range(4)
+        ]
+        chosen = jnp.logical_and(line >= at, line < at + 4)
+        kept = jnp.where(inside[None], 0.0, tiles)
+        kept = swapped(kept, tile, jnp.where(chosen, 0.0, kept[tile]))
+        lefts = [
+            swapped(
+                lefts[m], tile,
+                jnp.where(chosen, jnp.where(line == at + m, -1.0, 0.0), lefts[m][tile]),
             )
-            for n in range(4):
-                row = jnp.where(lane == k + n, small[m][n], row)
-            fresh.append(row)
-        inside = jnp.logical_and(lane >= k, lane < k + 4)
-        kept = jnp.where(inside[None], 0.0, tiles)
-        moved = kept - (
+            for m in range(4)
+        ]
+        tiles = kept - (
             (lefts[0] * fresh[0][None] + lefts[1] * fresh[1][None])
             + (lefts[2] * fresh[2][None] + lefts[3] * fresh[3][None])
         )
-        own = moved[tile]
-        for m in range(4):
-            own = jnp.where(line == at + m, fresh[m], own)
-        pieces = [own[None]]
-        if tile > 0:
-            pieces.insert(0, moved[:tile])
-        if tile < 15:
-            pieces.append(moved[tile + 1 :])
-        tiles = jnp.concatenate(pieces, axis=0)
     return tiles.reshape(128, 128)
 
 
-def invert_kernel(gram_ref, coarse_ref, parts_ref, start_ref, work):
+def invert(gram_ref, parts_ref, work):
     work[...] = gram_ref[...]
 
     @pl.loop(0, 3)
@@ -451,7 +484,6 @@
     parts_ref[0] = high
     parts_ref[1] = middle
     parts_ref[2] = low
-    start_ref[...] = solved(coarse_ref[...], parts_ref)
 
 
 def solved(right, parts_ref):
@@ -495,8 +527,17 @@
     return 4 * tile + lax.rem(tile, 4)
 
 
+def each_tile(act):
+    def some(step, _):
+        for j in range(4):
+            act(step * 4 + j)
+        return 0
+
+    lax.fori_loop(0, 4, some, 0)
+
+
 def reduce_start(pay, first_in, send, receive, own, plane):
-    def one(tile, _):
+    def one(tile):
         peer = owner_of(tile)
 
         @pl.when(peer != own)
@@ -505,9 +546,7 @@
                 pay.at[tile], first_in.at[own], send.at[tile], receive.at[own], peer, plane
             ).start()
 
-        return 0
-
-    lax.fori_loop(0, TILES, one, 0)
+    each_tile(one)
 
 
 def reduce_middle(pay, first_in, mid, second_in, last, result, sems, own, plane):
@@ -518,14 +557,13 @@
     def _():
         first_in[own] = pay[tile]
 
-        def one(i, _):
+        def one(i):
             peer = lax.rem(own + i, SUB)
             to_peer(
                 pay.at[tile], first_in.at[peer], send_1.at[tile], receive_1.at[peer], peer, plane
             ).wait_recv()
-            return 0
-
-        lax.fori_loop(1, SUB, one, 0)
+
+        each_peer(one)
         mid[...] = jnp.sum(first_in[...], axis=0)
         column(mid, second_in, send_2, receive_2, own, plane, "start")
         second_in[plane] = mid[...]
@@ -538,7 +576,7 @@
 def reduce_finish(pay, first_in, mid, second_in, last, result, sems, own, plane):
     send_1, receive_1, send_2, receive_2, send_3, receive_3 = sems
 
-    def one(tile, _):
+    def one(tile):
         peer = owner_of(tile)
 
         @pl.when(peer != own)
@@ -547,15 +585,13 @@
                 last, result.at[tile], send_3.at[peer], receive_3.at[tile], peer, plane
             ).wait_recv()
 
-        return 0
-
-    lax.fori_loop(0, TILES, one, 0)
+    each_tile(one)
 
 
 def reduce_sent(pay, first_in, mid, second_in, last, result, sems, own, plane):
     send_1, receive_1, send_2, receive_2, send_3, receive_3 = sems
 
-    def one(tile, _):
+    def one(tile):
         peer = owner_of(tile)
 
         @pl.when(peer != own)
@@ -564,9 +600,7 @@
                 pay.at[tile], first_in.at[own], send_1.at[tile], receive_1.at[own], peer, plane
             ).wait_send()
 
-        return 0
-
-    lax.fori_loop(0, TILES, one, 0)
+    each_tile(one)
     tile = own // 4
 
     @pl.when(lax.rem(own, 4) == lax.rem(tile, 4))
@@ -594,8 +628,8 @@
 
 def solve_kernel(
     residual_ref, modes_ref, mask_ref, own_ref, glued_ref, onehot_ref,
-    parts_ref, start_ref, coarse_ref, norm_ref,
-    multipliers_ref, amplitudes_ref,
+    gram_ref, coarse_ref, norm_ref,
+    multipliers_ref, amplitudes_ref, parts_ref, work,
     message, landed, pay_a, first_a, mid_a, second_a, last_a, result_a,
     pay_b, first_b, mid_b, second_b, last_b, result_b,
     send_x, receive_x,
@@ -612,7 +646,8 @@
 
     residual = residual_ref[...]
     coarse = coarse_ref[...]
-    start = start_ref[...]
+    invert(gram_ref, parts_ref, work)
+    start = solved(coarse, parts_ref)
     mask = mask_ref[...]
     own_row = own_ref[:1]
     direction = residual - expand(start, modes_ref, mask, own_row)
@@ -696,7 +731,7 @@
             shape((ROWS, ROWS), BF16), shape((ROWS, ROWS), BF16),
             shape((NC, NC)), shape((CASES, NC)), shape((CASES, 128)),
         ),
-        in_specs=[VMEM] * 5,
+        in_specs=[pl.BlockSpec(memory_space=pltpu.HBM)] * 5,
         out_specs=(VMEM,) * 9,
         scratch_shapes=[
             pltpu.VMEM((SUB, 8, 128), F32), pltpu.VMEM((SUB, 8, 128), F32),
@@ -707,6 +742,9 @@
             DMA((SUB,)), DMA((SUB,)), DMA((SUB,)), DMA((SUB,)),
             DMA((REP,)), DMA((REP,)), DMA((8,)), DMA((8,)),
             DMA((4,)), DMA((4,)), DMA((4,)), DMA((4,)),
+            pltpu.VMEM((1, ROWS, ROWS), BF16), pltpu.VMEM((MODES, 1, ROWS), F32),
+            pltpu.VMEM((1, ROWS), jnp.int32), pltpu.VMEM((1, SUB * REP), jnp.int32),
+            pltpu.VMEM((CASES, ROWS), F32), DMA((5,)),
         ],
         compiler_params=pltpu.CompilerParams(
             collective_id=0, has_side_effects=True, vmem_limit_bytes=LIMIT
@@ -719,31 +757,22 @@
         mode_block.reshape(1, SUB * REP),
         local_gap,
     )
-    parts, start = pl.pallas_call(
-        invert_kernel,
-        out_shape=(shape((3, NC, NC), BF16), shape((CASES, NC))),
-        in_specs=[VMEM] * 2,
-        out_specs=(VMEM,) * 2,
-        scratch_shapes=[pltpu.VMEM((NC, NC), F32)],
-        compiler_params=pltpu.CompilerParams(vmem_limit_bytes=LIMIT),
-        name="invert",
-    )(gram, coarse)
     tile = pltpu.VMEM((8, 128), F32)
     many = pltpu.VMEM((SUB, 8, 128), F32)
     few = pltpu.VMEM((TILES, 8, 128), F32)
     return pl.pallas_call(
         solve_kernel,
         out_shape=(shape((CASES, ROWS)), shape((CASES, NC))),
-        in_specs=[VMEM] * 10,
+        in_specs=[VMEM] * 9,
         out_specs=(VMEM,) * 2,
-        scratch_shapes=[many, many] + [few, many, tile, few, tile, few] * 2
+        scratch_shapes=[pltpu.VMEM((3, NC, NC), BF16), pltpu.VMEM((NC, NC), F32), many, many] + [few, many, tile, few, tile, few] * 2
         + [DMA((SUB,)), DMA((SUB,))]
         + [DMA((TILES,)), DMA((SUB,)), DMA((REP,)), DMA((REP,)), DMA((SUB,)), DMA((TILES,))] * 2,
         compiler_params=pltpu.CompilerParams(
             collective_id=1, has_side_effects=True, vmem_limit_bytes=LIMIT
         ),
         name="solve",
-    )(residual, modes, mask, own, glued, onehot, parts, start, coarse, norm)
+    )(residual, modes, mask, own, glued, onehot, gram, coarse, norm)
 
 
 def solution(mesh):

time: 166 us -> 159 us (0.958)
  Pallas kernels: 159 us -> 152 us
    pallas_call x1 -> x0, Pallas kernels: 29.5 us -> none  [body(): pl.pallas_call(invert_kernel, out_shape=(shape((3, NC, NC), BF16), shape(...]
    pallas_call x1, Pallas kernels: 59 us -> 80.6 us  [body(): pl.pallas_call(solve_kernel, out_shape=(shape((CASES, ROWS)), shape((CASE...]
where the time goes in v3:
time: 159 us; the launch traced here: 158 us
  Pallas kernels  152 us (96%)
  local copies, waits for them, and re-layouts  5.87 us (4%)
    pallas_call x1, Pallas kernels, body(): pl.pallas_call(solve_kernel, out_shape=(shape((CASES, ROWS)), shape((CASE...  80.6 us
    pallas_call x1, Pallas kernels, body(): pl.pallas_call(setup_kernel, out_shape=(shape((CASES, ROWS)), shape((2, 8...  71.1 us
    unnamed x12, local copies, waits for them, and re-layouts  5.87 us

profile of v3, /device:TPU:1, one launch (start us, length us, event | category | flops | bytes accessed | tf_op | source)
XLA Modules:
  0.0 158.3 jit_solution(7426521012385612841)
XLA Ops:
  0.6 0.0 copy-start
  0.6 1.6 copy-done
  2.2 0.0 copy-start.1
  2.2 0.9 copy-done.1
  3.1 0.0 copy-start.2
  3.1 0.7 copy-done.2
  3.9 0.0 copy-start.3
  3.9 0.7 copy-done.3
  4.6 0.0 copy-start.4
  4.6 0.7 copy-done.4
  5.2 71.1 %setup.1 = (f32[32,1024]{1,0:T(8,128)S(1)}, f32[2,8,1024]{2,1,0:T(8,128)S(1)}, bf16[128,1024]{1,0:T(8,128)(2,1)S(1)}, f32[8,128]{1,0:T(8,128)S(1)}, bf16[1024,10...) custom-call(bf16[1,1024,1024]{2,1,0:T(8,128)(2,1)S(1)} %copy-done, ...), custom_call_target="tpu_custom_call" | custom-call | tf_op jit(solution)/shard_map/setup/pallas_call | solution.py:727
  76.3 80.6 %solve.1 = (f32[32,1024]{1,0:T(8,128)S(1)}, f32[32,384]{1,0:T(8,128)S(1)}) custom-call(f32[32,1024]{1,0:T(8,128)S(1)} %get-tuple-element.11.residual_ref, f32[2,8,1024]{2,1,0:T(8,128)S(1)} %get-tuple-element.12.modes_ref, bf16[128,1024]{1,0:T(8,128)(2,1)S(1)} %get-tuple-element.13.mask_ref, f32[8,128]{1,0:T(8,128)S(1)} %get-tuple-element.14.own_ref, ...), custom_call_target="tpu_custom_call" | custom-call | tf_op jit(solution)/shard_map/solve/pallas_call | solution.py:763
  157.0 0.7 copy.9
  157.6 0.6 copy.10
Async XLA Ops:
  0.6 1.6 %copy-start = (bf16[1,1024,1024]{2,1,0:T(8,128)(2,1)S(1)}, bf16[1,1024,1024]{2,1,0:T(8,128)(2,1)}, u32[]{:S(2)}) copy-start(bf16[1,1024,1024]{2,1,0:T(8,128)(2,1)} %operator_in.1) | copy-start | bytes 6291460
  2.2 0.9 copy-start.1
  3.1 0.7 copy-start.2
  3.9 0.7 copy-start.3
  4.6 0.7 copy-start.4

commit v4 on v3

--- a/solution.py
+++ b/solution.py
@@ -16,7 +16,7 @@
 TILES = 16
 SLICE = 24
 HALF = 24
-LIMIT = 24 * 1024 * 1024
+LIMIT = 60 * 1024 * 1024
 F32 = jnp.float32
 BF16 = jnp.bfloat16
 HIGHEST = lax.Precision.HIGHEST
@@ -412,6 +412,12 @@
     return jnp.concatenate(pieces, axis=0)
 
 
+def picked(values, chosen):
+    return jnp.broadcast_to(
+        jnp.sum(jnp.where(chosen, values, 0.0), axis=0, keepdims=True), (8, 128)
+    )
+
+
 def invert_block(pivot):
     tiles = pivot.reshape(16, 8, 128)
     lane = iota((8, 128), 1)
@@ -425,7 +431,7 @@
             jnp.broadcast_to(tiles[tile, at + m : at + m + 1, :], (8, 128)) for m in range(4)
         ]
         small = [
-            [jnp.broadcast_to(lefts[n][tile, at + m : at + m + 1, :], (8, 128)) for n in range(4)]
+            [picked(lefts[n][tile], line == at + m) for n in range(4)]
             for m in range(4)
         ]
         for p in range(4):
@@ -638,7 +644,6 @@
 ):
     own = lax.axis_index("sub")
     plane = lax.axis_index("rep")
-    barrier = greet(own, plane)
     round_a = (pay_a, first_a, mid_a, second_a, last_a, result_a,
                (send_a1, receive_a1, send_a2, receive_a2, send_a3, receive_a3), own, plane)
     round_b = (pay_b, first_b, mid_b, second_b, last_b, result_b,
@@ -660,7 +665,6 @@
         (2.0 * row_sum(direction * product),),
     )
 
-    pl.semaphore_wait(barrier, SUB - 1 + REP - 1)
     reduce_start(pay_a, first_a, send_a1, receive_a1, own, plane)
     exchange_start(message, landed, send_x, receive_x, own, plane)
     flip_own(message, landed, own)
@@ -723,33 +727,53 @@
     return jax.ShapeDtypeStruct(dims, kind)
 
 
+def whole_kernel(*refs):
+    inputs, outputs = refs[:5], refs[5:7]
+    between, setup_work, solve_work = refs[7:16], refs[16:44], refs[44:]
+    setup_kernel(*inputs, *between, *setup_work)
+    solve_kernel(*between, *outputs, *solve_work)
+
+
 def body(dual_ops, mode_traces, route, mode_block, local_gap):
-    residual, modes, mask, own, glued, onehot, gram, coarse, norm = pl.pallas_call(
-        setup_kernel,
-        out_shape=(
-            shape((CASES, ROWS)), shape((2, 8, ROWS)), shape((128, ROWS), BF16), shape((8, 128)),
-            shape((ROWS, ROWS), BF16), shape((ROWS, ROWS), BF16),
-            shape((NC, NC)), shape((CASES, NC)), shape((CASES, 128)),
-        ),
+    tile = pltpu.VMEM((8, 128), F32)
+    many = pltpu.VMEM((SUB, 8, 128), F32)
+    few = pltpu.VMEM((TILES, 8, 128), F32)
+    between = [
+        pltpu.VMEM((CASES, ROWS), F32), pltpu.VMEM((2, 8, ROWS), F32),
+        pltpu.VMEM((128, ROWS), BF16), pltpu.VMEM((8, 128), F32),
+        pltpu.VMEM((ROWS, ROWS), BF16), pltpu.VMEM((ROWS, ROWS), BF16),
+        pltpu.VMEM((NC, NC), F32), pltpu.VMEM((CASES, NC), F32), pltpu.VMEM((CASES, 128), F32),
+    ]
+    setup_work = [
+        many, many,
+        pltpu.VMEM((ROWS, ROWS), BF16), pltpu.VMEM((ROWS, ROWS), BF16),
+        pltpu.VMEM((AGGS, 1, 128), F32), pltpu.VMEM((SUB, 1, 128), F32),
+        pltpu.VMEM((SLICE, 128), F32), pltpu.VMEM((REP, SLICE, 128), F32),
+        pltpu.VMEM((SLICE, 128), F32), pltpu.VMEM((AGGS, SLICE, 128), F32),
+        DMA((SUB,)), DMA((SUB,)), DMA((SUB,)), DMA((SUB,)),
+        DMA((REP,)), DMA((REP,)), DMA((8,)), DMA((8,)),
+        DMA((4,)), DMA((4,)), DMA((4,)), DMA((4,)),
+        pltpu.VMEM((1, ROWS, ROWS), BF16), pltpu.VMEM((MODES, 1, ROWS), F32),
+        pltpu.VMEM((1, ROWS), jnp.int32), pltpu.VMEM((1, SUB * REP), jnp.int32),
+        pltpu.VMEM((CASES, ROWS), F32), DMA((5,)),
+    ]
+    solve_work = (
+        [pltpu.VMEM((3, NC, NC), BF16), pltpu.VMEM((NC, NC), F32), many, many]
+        + [few, many, tile, few, tile, few] * 2
+        + [DMA((SUB,)), DMA((SUB,))]
+        + [DMA((TILES,)), DMA((SUB,)), DMA((REP,)), DMA((REP,)), DMA((SUB,)), DMA((TILES,))] * 2
+    )
+    assert len(setup_work) == 28
+    return pl.pallas_call(
+        whole_kernel,
+        out_shape=(shape((CASES, ROWS)), shape((CASES, NC))),
         in_specs=[pl.BlockSpec(memory_space=pltpu.HBM)] * 5,
-        out_specs=(VMEM,) * 9,
-        scratch_shapes=[
-            pltpu.VMEM((SUB, 8, 128), F32), pltpu.VMEM((SUB, 8, 128), F32),
-            pltpu.VMEM((ROWS, ROWS), BF16), pltpu.VMEM((ROWS, ROWS), BF16),
-            pltpu.VMEM((AGGS, 1, 128), F32), pltpu.VMEM((SUB, 1, 128), F32),
-            pltpu.VMEM((SLICE, 128), F32), pltpu.VMEM((REP, SLICE, 128), F32),
-            pltpu.VMEM((SLICE, 128), F32), pltpu.VMEM((AGGS, SLICE, 128), F32),
-            DMA((SUB,)), DMA((SUB,)), DMA((SUB,)), DMA((SUB,)),
-            DMA((REP,)), DMA((REP,)), DMA((8,)), DMA((8,)),
-            DMA((4,)), DMA((4,)), DMA((4,)), DMA((4,)),
-            pltpu.VMEM((1, ROWS, ROWS), BF16), pltpu.VMEM((MODES, 1, ROWS), F32),
-            pltpu.VMEM((1, ROWS), jnp.int32), pltpu.VMEM((1, SUB * REP), jnp.int32),
-            pltpu.VMEM((CASES, ROWS), F32), DMA((5,)),
-        ],
+        out_specs=(VMEM,) * 2,
+        scratch_shapes=between + setup_work + solve_work,
         compiler_params=pltpu.CompilerParams(
             collective_id=0, has_side_effects=True, vmem_limit_bytes=LIMIT
         ),
-        name="setup",
+        name="whole",
     )(
         dual_ops,
         jnp.transpose(mode_traces, (1, 0, 2)),
@@ -757,22 +781,6 @@
         mode_block.reshape(1, SUB * REP),
         local_gap,
     )
-    tile = pltpu.VMEM((8, 128), F32)
-    many = pltpu.VMEM((SUB, 8, 128), F32)
-    few = pltpu.VMEM((TILES, 8, 128), F32)
-    return pl.pallas_call(
-        solve_kernel,
-        out_shape=(shape((CASES, ROWS)), shape((CASES, NC))),
-        in_specs=[VMEM] * 9,
-        out_specs=(VMEM,) * 2,
-        scratch_shapes=[pltpu.VMEM((3, NC, NC), BF16), pltpu.VMEM((NC, NC), F32), many, many] + [few, many, tile, few, tile, few] * 2
-        + [DMA((SUB,)), DMA((SUB,))]
-        + [DMA((TILES,)), DMA((SUB,)), DMA((REP,)), DMA((REP,)), DMA((SUB,)), DMA((TILES,))] * 2,
-        compiler_params=pltpu.CompilerParams(
-            collective_id=1, has_side_effects=True, vmem_limit_bytes=LIMIT
-        ),
-        name="solve",
-    )(residual, modes, mask, own, glued, onehot, gram, coarse, norm)
 
 
 def solution(mesh):

time: 159 us -> 143 us (0.90)
  Pallas kernels: 152 us -> 139 us
  local copies, waits for them, and re-layouts: 5.87 us -> 2.99 us
    pallas_call x2 -> x1, Pallas kernels: 152 us -> 139 us  [body(): pl.pallas_call(whole_kernel, out_shape=(shape((CASES, ROWS)), shape((CASE...]
    unnamed x12 -> x2, local copies, waits for them, and re-layouts: 5.87 us -> 2.99 us
where the time goes in v4:
time: 143 us
  Pallas kernels  139 us (97%)
  local copies, waits for them, and re-layouts  2.99 us (2%)
    pallas_call x1, Pallas kernels, body(): pl.pallas_call(whole_kernel, out_shape=(shape((CASES, ROWS)), shape((CASE...  139 us
    unnamed x2, local copies, waits for them, and re-layouts  2.99 us

profile of v4, /device:TPU:1, one launch (start us, length us, event | category | flops | bytes accessed | tf_op | source)
XLA Modules:
  0.0 142.7 jit_solution(6467569154446184197)
XLA Ops:
  0.6 139.1 %whole.1 = (f32[32,1024]{1,0:T(8,128)}, f32[32,384]{1,0:T(8,128)}) custom-call(bf16[1,1024,1024]{2,1,0:T(8,128)(2,1)} %refs_0_.1, f32[6,1,1024]{2,1,0:T(1,128)} %bitcast.2, s32[1,1024]{1,0:T(1,128)} %refs_2_.1, s32[1,1024]{1,0:T(1,128)} %bitcast.3, f32[32,1024]{1,0:T(8,128)} %refs_4_.1), custom_call_target="tpu_custom_call" | custom-call | tf_op jit(solution)/shard_map/whole/pallas_call | solution.py:767
  139.7 1.6 %copy.9 = f32[32,1024]{1,0:T(8,128)} copy(f32[32,1024]{1,0:T(8,128)} %get-tuple-element.4) | data formatting | bytes 262144
  141.3 1.4 copy.10
